TPU v7x, 512 devices: a whole 4x4x16 slice. The times are simulated.
512 devices in a mesh: bucket: 128 (over x, z, core), rerank: 4 (over y).
Axes of the slice: x: 4, y: 4, z: 16, core: 2. Of those that a mesh axis runs over, the one named last changes fastest.
Arguments:
- queries: bfloat16 [32768, 768], P(('bucket', 'rerank')), may hold values from -6 to 6
- class_in: bfloat16 [768, 1024], replicated, may hold values from -0.21875 to 0.21875
- class_out: bfloat16 [1024, 262144], P(None, ('bucket', 'rerank')), may hold values from -0.1875 to 0.1875
- passages: bfloat16 [393216, 768], P(('bucket', 'rerank')), may hold values from -0.19921875 to 0.19921875
- bucket_sizes: int32 [512, 512], P(('bucket', 'rerank')), may hold values from 1 to 8, 768 in all within a row
- bucket_owner: int32 [32768, 8], P(('bucket', 'rerank')), may hold values from 0 to 511, all different within a row; in each aligned block of 64 rows (0 to 63, 64 to 127, ...) at most 2 rows name the same one
- bucket_slot: int32 [32768, 8], P(('bucket', 'rerank')), may hold values from 0 to 511
- embed: bfloat16 [32768, 4096], P('bucket', 'rerank'), may hold values from -6 to 6
- w_gate: bfloat16 [4096, 14336], P('rerank', 'bucket'), may hold values from -0.09375 to 0.09375
- w_up: bfloat16 [4096, 14336], P('rerank', 'bucket'), may hold values from -0.09375 to 0.09375
- w_score: bfloat16 [14336], P('bucket'), may hold values from -0.046875 to 0.046875
- block_tokens: int32 [4, 128], replicated, may hold values from 0 to 32767
Outputs:
- bucket_logit: float32 [32768, 8], P(('bucket', 'rerank'))
- bucket_mass: float32 [32768, 8], P(('bucket', 'rerank'))
- token_scores: float32 [4, 128], P('rerank')
Inputs may be any that keep to these rules, and one draw needn't show every extreme that they name: `bucket_owner`: each query names 8 different owner devices, numbered bucket index times the rerank axis's size plus rerank index; within the 64 queries of one device no owner is named more than 2 times, and that many in some devices. `bucket_sizes`: the sizes of one device's 512 buckets sum to 768.
All inputs are finite; a program needn't handle non-finite values.
Results may differ from a plain program's by a relative error of at most 0.0029.
Values may be sent and summed in bfloat16 or wider, within the bound.
A program may use at most 64 MiB of HBM per device.

v0:
```python
import jax
import jax.numpy as jnp
from jax import lax
from jax.sharding import PartitionSpec as P


def body(
    queries,
    class_in,
    class_out,
    passages,
    bucket_sizes,
    bucket_owner,
    bucket_slot,
    embed,
    w_gate,
    w_up,
    w_score,
    block_tokens,
):
    groups = lax.axis_size("bucket")
    rank_count = lax.axis_size("rerank")
    devices = groups * rank_count
    query_rows, top_count = bucket_owner.shape
    capacity = max(2, 2 * query_rows * top_count // devices)
    pair_count = query_rows * top_count
    total_slots = devices * capacity
    width = queries.shape[1]
    owner_flat = bucket_owner.reshape(pair_count)
    slot_flat = bucket_slot.reshape(pair_count)
    pair_order = jnp.arange(pair_count, dtype=jnp.int32)
    earlier = (owner_flat[:, None] == owner_flat[None, :]) & (
        pair_order[None, :] < pair_order[:, None]
    )
    rank_in = jnp.sum(earlier.astype(jnp.int32), axis=1)
    target = owner_flat * capacity + rank_in
    source_row = pair_order // top_count
    send_queries = (
        jnp.zeros((total_slots, width), jnp.bfloat16)
        .at[target]
        .set(jnp.take(queries, source_row, axis=0))
    )
    send_queries = send_queries.reshape(groups, rank_count, capacity, width)
    send_slots = (
        jnp.full((total_slots,), -1, jnp.int32)
        .at[target]
        .set(slot_flat)
        .reshape(groups, rank_count, capacity)
    )
    hidden = jax.nn.relu(jnp.dot(queries, class_in, preferred_element_type=jnp.float32)).astype(
        jnp.bfloat16
    )
    hidden_width = hidden.shape[1]
    send_hidden = (
        jnp.zeros((total_slots, hidden_width), jnp.bfloat16)
        .at[target]
        .set(jnp.take(hidden, source_row, axis=0))
    )
    send_hidden = send_hidden.reshape(groups, rank_count, capacity, hidden_width)
    got_queries, got_hidden, got_slots = (
        lax.all_to_all(
            lax.all_to_all(send_queries, "bucket", split_axis=0, concat_axis=0, tiled=True),
            "rerank",
            split_axis=1,
            concat_axis=1,
            tiled=True,
        ),
        lax.all_to_all(
            lax.all_to_all(send_hidden, "bucket", split_axis=0, concat_axis=0, tiled=True),
            "rerank",
            split_axis=1,
            concat_axis=1,
            tiled=True,
        ),
        lax.all_to_all(
            lax.all_to_all(send_slots, "bucket", split_axis=0, concat_axis=0, tiled=True),
            "rerank",
            split_axis=1,
            concat_axis=1,
            tiled=True,
        ),
    )
    got_queries = got_queries.reshape(total_slots, width)
    got_hidden = got_hidden.reshape(total_slots, hidden_width)
    got_slots = got_slots.reshape(total_slots)
    columns = jnp.arange(class_out.shape[1], dtype=jnp.int32)
    all_logits = jnp.dot(got_hidden, class_out, preferred_element_type=jnp.float32)
    slot_logit = jnp.sum(jnp.where(got_slots[:, None] == columns[None, :], all_logits, 0.0), axis=1)
    bucket_len = bucket_sizes.reshape(-1)
    bucket_end = jnp.cumsum(bucket_len)
    positions = jnp.arange(passages.shape[0], dtype=jnp.int32)
    passage_bucket = jnp.sum((bucket_end[:, None] <= positions[None, :]).astype(jnp.int32), axis=0)
    similar = jnp.einsum("sd,pd->sp", got_queries, passages, preferred_element_type=jnp.float32)
    slot_mass = jnp.sum(
        jnp.where(got_slots[:, None] == passage_bucket[None, :], jnp.exp(similar), 0.0), axis=1
    )
    back_logit, back_mass = (
        lax.all_to_all(
            lax.all_to_all(
                slot_logit.reshape(groups, rank_count, capacity),
                "bucket",
                split_axis=0,
                concat_axis=0,
                tiled=True,
            ),
            "rerank",
            split_axis=1,
            concat_axis=1,
            tiled=True,
        ),
        lax.all_to_all(
            lax.all_to_all(
                slot_mass.reshape(groups, rank_count, capacity),
                "bucket",
                split_axis=0,
                concat_axis=0,
                tiled=True,
            ),
            "rerank",
            split_axis=1,
            concat_axis=1,
            tiled=True,
        ),
    )
    bucket_logit = jnp.take(back_logit.reshape(total_slots), target).reshape(query_rows, top_count)
    bucket_mass = jnp.take(back_mass.reshape(total_slots), target).reshape(query_rows, top_count)
    vocab_rows = embed.shape[0]
    tokens = block_tokens.reshape(-1)
    local_ids = tokens - lax.axis_index("bucket") * vocab_rows
    vocab_ids = jnp.arange(vocab_rows, dtype=jnp.int32)
    token_picks = (local_ids[:, None] == vocab_ids[None, :]).astype(jnp.bfloat16)
    partial_rows = jnp.dot(token_picks, embed, preferred_element_type=jnp.float32)
    token_rows = lax.psum(partial_rows, "bucket").astype(jnp.bfloat16)
    gate_part = jnp.dot(token_rows, w_gate, preferred_element_type=jnp.float32)
    up_part = jnp.dot(token_rows, w_up, preferred_element_type=jnp.float32)
    share_rows = tokens.shape[0] // rank_count
    gate_all, up_all = lax.psum((gate_part, up_part), "rerank")
    share_start = lax.axis_index("rerank") * share_rows
    gate_share = lax.dynamic_slice_in_dim(gate_all, share_start, share_rows, 0)
    up_share = lax.dynamic_slice_in_dim(up_all, share_start, share_rows, 0)
    mixed_rows = jax.nn.silu(gate_share) * up_share
    partial_value = jnp.dot(
        mixed_rows, w_score.astype(jnp.float32), precision=lax.Precision.HIGHEST
    )
    partial_value = partial_value.reshape(
        block_tokens.shape[0] // rank_count, block_tokens.shape[1]
    )
    token_scores = lax.psum(partial_value, "bucket")
    return (bucket_logit, bucket_mass, token_scores)


def solution(mesh):
    placed = (
        P(("bucket", "rerank"), None),
        P(),
        P(None, ("bucket", "rerank")),
        P(("bucket", "rerank"), None),
        P(("bucket", "rerank"), None),
        P(("bucket", "rerank"), None),
        P(("bucket", "rerank"), None),
        P("bucket", "rerank"),
        P("rerank", "bucket"),
        P("rerank", "bucket"),
        P("bucket"),
        P(),
    )
    return jax.shard_map(
        body,
        mesh=mesh,
        in_specs=placed,
        out_specs=(P(("bucket", "rerank"), None), P(("bucket", "rerank"), None), P("rerank", None)),
        check_vma=False,
    )
```

profile of v0, /device:TPU:1, one launch (start us, length us, event | category | flops | bytes accessed | tf_op | source)
XLA Modules:
  0.0 1139.1 jit_solution(12211933795051451154)
XLA Ops:
  10.2 2.4 scatter_custom_fusion
  14.4 20.4 %all-to-all-start = ((s32[128,4,2]{1,2,0:T(2,128)}), s32[128,4,2]{1,2,0:T(2,128)S(1)}, u32[]{:S(2)}, u32[]{:S(2)}) async-start(s32[128,4,2]{1,2,0:T(2,128)} %copy.55), calls=%async_computation | async-start | bytes 262144 | tf_op jit(solution)/shard_map/all_to_all | solution.py:76
  34.9 7.2 scatter_custom_fusion.2
  43.6 8.6 all-to-all-done
  52.2 8.2 all-to-all-start.6
  61.1 76.0 %all-to-all-done.6 = bf16[128,4,2,768]{3,2,1,0:T(2,128)(2,1)S(1)} async-done(((bf16[128,4,2,768]{3,2,1,0:T(2,128)(2,1)}), bf16[128,4,2,768]{3,2,1,0:T(2,128)(2,1)S(1)}, u32[]{:S(2)}, u32[]{:S(2)}) %all-to-all-start.6) | async-done | bytes 1572896 | tf_op jit(solution)/shard_map/all_to_all | solution.py:62
  137.1 4.2 all-to-all-start.1
  145.4 3.6 all-to-all-start.7
  149.4 7.8 scatter_custom_fusion.1
  157.2 4.1 reshape.167
  161.3 6.0 all-to-all-done.7
  167.3 11.9 %all-to-all-start.2 = ((bf16[128,4,2,1024]{3,2,1,0:T(2,128)(2,1)}), bf16[128,4,2,1024]{3,2,1,0:T(2,128)(2,1)}, u32[]{:S(2)}, u32[]{:S(2)}) async-start(bf16[128,4,2,1024]{3,2,1,0:T(2,128)(2,1)} %reshape.167), calls=%async_computation.2 | async-start | bytes 4194304 | tf_op jit(solution)/shard_map/all_to_all | solution.py:69
  182.7 3.7 reshape.175
  186.4 2.8 select_reduce_fusion
  191.0 86.8 %all-to-all-done.2 = bf16[128,4,2,1024]{3,2,1,0:T(2,128)(2,1)} async-done(((bf16[128,4,2,1024]{3,2,1,0:T(2,128)(2,1)}), bf16[128,4,2,1024]{3,2,1,0:T(2,128)(2,1)}, u32[]{:S(2)}, u32[]{:S(2)}) %all-to-all-start.2) | async-done | bytes 2097184 | tf_op jit(solution)/shard_map/all_to_all | solution.py:69
  277.8 8.7 all-to-all-start.8
  286.5 2.9 fusion.15
  289.3 4.4 copy.58
  293.7 10.2 all-to-all-done.8
  303.9 4.4 all-to-all-start.3
  308.4 505.3 %all-reduce.5 = bf16[512,1024]{1,0:T(8,128)(2,1)S(1)} all-reduce(f32[512,1024]{1,0:T(8,128)} %fusion.15), channel_id=1, replica_groups=mesh['bucket'=128,'rerank'=4] {'bucket'}, use_global_device_ids=true, to_apply=%region_9.11 | all-reduce | flops 524288 | bytes 3145728 | tf_op jit(solution)/shard_map/psum | solution.py:133
  816.8 4.3 all-to-all-start.9
  821.2 5.3 copy.59
  826.5 4.2 reshape.168
  830.7 2.9 select_reduce_fusion.1
  835.5 11.2 all-to-all-start.4
  846.7 20.2 %all-reduce.4.cloned.1.call-done = (f32[512,112]{0,1:T(8,128)}, f32[512,112]{0,1:T(8,128)}) async-done(((f32[512,112]{0,1:T(8,128)}, f32[512,112]{0,1:T(8,128)}), (f32[512,112]{0,1:T(8,128)}, f32[512,112]{0,1:T(8,128)})) %all-reduce.4.cloned.1.call-update) | async-done | bytes 458768 | tf_op jit(solution)/shard_map/psum | solution.py:137
  867.8 249.9 %psum.31 = f32[1,128]{1,0:T(1,128)} all-reduce(f32[1,128]{1,0:T(1,128)S(1)} %fusion.18), channel_id=1, replica_groups=mesh['bucket'=128,'rerank'=4] {'bucket'}, use_global_device_ids=true, to_apply=%region_12.14 | all-reduce | flops 128 | bytes 1024 | tf_op jit(solution)/shard_map/psum | solution.py:148
  1118.2 2.3 gather_fusion.1
  1121.1 3.3 all-to-all-start.5
  1125.2 3.4 all-to-all-done.5
  1129.0 2.3 gather_fusion
  (71 shorter events, 25.9 us)
Async XLA Ops:
  7.2 141.8 %copy-start = (bf16[768,1024]{1,0:T(8,128)(2,1)S(1)}, bf16[768,1024]{1,0:T(8,128)(2,1)}, u32[]{:S(2)}) copy-start(bf16[768,1024]{1,0:T(8,128)(2,1)} %param.15) | copy-start | bytes 4718596
  14.4 37.8 %all-to-all-start = ((s32[128,4,2]{1,2,0:T(2,128)}), s32[128,4,2]{1,2,0:T(2,128)S(1)}, u32[]{:S(2)}, u32[]{:S(2)}) async-start(s32[128,4,2]{1,2,0:T(2,128)} %copy.55), calls=%async_computation | async-start | bytes 262144 | tf_op jit(solution)/shard_map/all_to_all | solution.py:76
  52.2 84.9 %all-to-all-start.6 = ((bf16[128,4,2,768]{3,2,1,0:T(2,128)(2,1)}), bf16[128,4,2,768]{3,2,1,0:T(2,128)(2,1)S(1)}, u32[]{:S(2)}, u32[]{:S(2)}) async-start(bf16[128,4,2,768]{3,2,1,0:T(2,128)(2,1)} %reshape.174), calls=%async_computation.6 | async-start | bytes 3145728 | tf_op jit(solution)/shard_map/all_to_all | solution.py:62
  137.1 8.3 all-to-all-start.1
  143.5 5.5 copy-start.1
  145.4 21.9 %all-to-all-start.7 = ((bf16[128,4,2,768]{3,2,0,1:T(2,128)(2,1)}), bf16[128,4,2,768]{3,2,0,1:T(2,128)(2,1)S(1)}, u32[]{:S(2)}, u32[]{:S(2)}) async-start(bf16[128,4,2,768]{3,2,0,1:T(2,128)(2,1)} %copy.63), calls=%async_computation.7 | async-start | bytes 3145728 | tf_op jit(solution)/shard_map/all_to_all | solution.py:61
  161.3 17.9 %copy-start.4 = (s32[1,512]{1,0:T(1,128)S(1)}, s32[1,512]{1,0:T(1,128)}, u32[]{:S(2)}) copy-start(s32[1,512]{1,0:T(1,128)} %param.18) | copy-start | bytes 6148
  161.3 18.7 %copy-start.5 = (s32[4,128]{1,0:T(4,128)S(1)}, s32[4,128]{1,0:T(4,128)}, u32[]{:S(2)}) copy-start(s32[4,128]{1,0:T(4,128)} %param.25) | copy-start | bytes 6148
  167.3 110.5 %all-to-all-start.2 = ((bf16[128,4,2,1024]{3,2,1,0:T(2,128)(2,1)}), bf16[128,4,2,1024]{3,2,1,0:T(2,128)(2,1)}, u32[]{:S(2)}, u32[]{:S(2)}) async-start(bf16[128,4,2,1024]{3,2,1,0:T(2,128)(2,1)} %reshape.167), calls=%async_computation.2 | async-start | bytes 4194304 | tf_op jit(solution)/shard_map/all_to_all | solution.py:69
  277.8 26.1 %all-to-all-start.8 = ((f32[128,4,2]{1,2,0:T(2,128)}), f32[128,4,2]{1,2,0:T(2,128)S(1)}, u32[]{:S(2)}, u32[]{:S(2)}) async-start(f32[128,4,2]{1,2,0:T(2,128)} %copy.65), calls=%async_computation.8 | async-start | bytes 262144 | tf_op jit(solution)/shard_map/all_to_all | solution.py:112
  303.9 512.9 %all-to-all-start.3 = ((bf16[128,4,2,1024]{3,2,0,1:T(2,128)(2,1)}), bf16[128,4,2,1024]{3,2,0,1:T(2,128)(2,1)}, u32[]{:S(2)}, u32[]{:S(2)}) async-start(bf16[128,4,2,1024]{3,2,0,1:T(2,128)(2,1)} %copy.58), calls=%async_computation.3 | async-start | bytes 4194304 | tf_op jit(solution)/shard_map/all_to_all | solution.py:68
  308.4 505.4 %copy-start.2 = (bf16[1024,112]{0,1:T(8,128)(2,1)S(1)}, bf16[1024,112]{0,1:T(8,128)(2,1)}, u32[]{:S(2)}) copy-start(bf16[1024,112]{0,1:T(8,128)(2,1)} %param.23) | copy-start | bytes 688132
  308.4 506.6 %copy-start.3 = (bf16[1024,112]{0,1:T(8,128)(2,1)S(1)}, bf16[1024,112]{0,1:T(8,128)(2,1)}, u32[]{:S(2)}) copy-start(bf16[1024,112]{0,1:T(8,128)(2,1)} %param.22) | copy-start | bytes 688132
  308.4 558.5 %all-reduce.4.cloned.1.call-start = ((), (), s32[]{:S(2)}) async-start(), calls=%async_computation.10 | async-start | bytes 917504 | tf_op jit(solution)/shard_map/psum | solution.py:137
  816.8 18.6 %all-to-all-start.9 = ((f32[128,4,2]{0,2,1:T(2,128)}), f32[128,4,2]{0,2,1:T(2,128)S(1)}, u32[]{:S(2)}, u32[]{:S(2)}) async-start(f32[128,4,2]{0,2,1:T(2,128)} %copy.66), calls=%async_computation.9 | async-start | bytes 8192 | tf_op jit(solution)/shard_map/all_to_all | solution.py:111
  826.5 4.2 copy-start.6
  830.7 36.1 %copy-start.7 = (bf16[112]{0:T(256)(128)(2,1)S(1)}, bf16[112]{0:T(256)(128)(2,1)}, u32[]{:S(2)}) copy-start(bf16[112]{0:T(256)(128)(2,1)} %param.24) | copy-start | bytes 676
  835.5 285.0 %all-to-all-start.4 = ((f32[128,4,2]{1,2,0:T(2,128)}), f32[128,4,2]{1,2,0:T(2,128)S(1)}, u32[]{:S(2)}, u32[]{:S(2)}) async-start(f32[128,4,2]{1,2,0:T(2,128)} %copy.60), calls=%async_computation.4 | async-start | bytes 262144 | tf_op jit(solution)/shard_map/all_to_all | solution.py:99
  1121.1 7.4 all-to-all-start.5
Sparse Core Ops, SparseCore 0:
  816.3 50.5 all-reduce.3
where the time goes:
time: 1150 us; the launch traced here: 1140 us
  blocking collectives  755 us (66%)
  waiting for transfers between devices  213 us (19%)
  starting transfers between devices  80.2 us (7%)
  local copies, waits for them, and re-layouts  47.2 us (4%)
  other arithmetic  16.6 us (1%)
  between operations  14.6 us (1%)
  matrix products  12.3 us (1%)
    psum x1, blocking collectives, body(): token_rows = lax.psum(partial_rows, 'bucket').astype(jnp.bfloat16)  505 us
    psum x1, blocking collectives, body(): token_scores = lax.psum(partial_value, 'bucket')  250 us
    all_to_all x1, waiting for transfers between devices, body(): lax.all_to_all(send_hidden, 'bucket', split_axis=0, concat_axis=0, tiled=...  86.8 us
    all_to_all x1, waiting for transfers between devices, body(): lax.all_to_all(send_queries, 'bucket', split_axis=0, concat_axis=0, tiled...  76 us
  transfers between devices with their start and end apart: 11, of which 8 were waited for; matrix products, arithmetic and copies ran while one was open for 6% of the time, Pallas kernels for 0%

commit v1 on v0

v1 whole, which is shorter than its diff:
```python
import functools

import jax
import jax.numpy as jnp
from jax import lax
from jax.experimental import pallas as pl
from jax.experimental.pallas import tpu as pltpu
from jax.sharding import Mesh, PartitionSpec as P

AXES = ("x", "z", "c", "y")
NX, NZ, NC, NY = 4, 16, 2, 4
NO = NX * NC * NY
BF = jnp.bfloat16
F32 = jnp.float32
VM = pl.BlockSpec(memory_space=pltpu.VMEM)


def here():
    return tuple(lax.axis_index(a) for a in AXES)


def remote(src, dst, send, recv, device):
    return pltpu.make_async_remote_copy(
        src_ref=src,
        dst_ref=dst,
        send_sem=send,
        recv_sem=recv,
        device_id=device,
        device_id_type=pl.DeviceIdType.MESH,
    )


def greet(peers_of, count):
    barrier = pltpu.get_barrier_semaphore()

    @pl.loop(1, count)
    def _(k):
        device, _ = peers_of(k)
        pl.semaphore_signal(barrier, inc=1, device_id=device, device_id_type=pl.DeviceIdType.MESH)


def plane_peer(k):
    x, z, c, y = here()
    px = lax.rem(x + k // (NC * NY), NX)
    pc = lax.rem(c + lax.rem(k // NY, NC), NC)
    py = lax.rem(y + lax.rem(k, NY), NY)
    return (px, z, pc, py), (px * NC + pc) * NY + py


def side_peer(k):
    x, z, c, y = here()
    px = lax.rem(x + k // NC, NX)
    pc = lax.rem(c + lax.rem(k, NC), NC)
    return (px, z, pc, y), px * NC + pc


def line_peer(k):
    x, z, c, y = here()
    pz = lax.rem(z + k, NZ)
    return (x, pz, c, y), pz


def row_peer(k):
    x, z, c, y = here()
    py = lax.rem(y + k, NY)
    return (x, z, c, py), py


def line_gather(q_ref, i_ref, out_ref, iout_ref, send_sem, recv_sem):
    x, z, c, y = here()
    right = (x, lax.rem(z + 1, NZ), c, y)
    left = (x, lax.rem(z + NZ - 1, NZ), c, y)
    barrier = pltpu.get_barrier_semaphore()
    for device in (left, right):
        pl.semaphore_signal(barrier, inc=1, device_id=device, device_id_type=pl.DeviceIdType.MESH)
    pl.semaphore_wait(barrier, 2)

    def copy(way, step, part):
        place = lax.rem(z + (NZ - step if way == 0 else step), NZ)
        device = right if way == 0 else left
        if part < 2:
            src = q_ref.at[part] if step == 0 else out_ref.at[place, part]
            dst = out_ref.at[place, part]
        else:
            src = i_ref if step == 0 else iout_ref.at[place]
            dst = iout_ref.at[place]
        return remote(src, dst, send_sem.at[way, step, part], recv_sem.at[way, step, part], device)

    started = {}
    for step in range(NZ // 2):
        for part in (2, 0, 1):
            for way in (0, 1):
                if step > 0 and (way, step - 1, part) in started:
                    started[way, step - 1, part].wait_recv()
                if way == 1 and step == NZ // 2 - 1:
                    continue
                started[way, step, part] = copy(way, step, part)
                started[way, step, part].start()
        if step == 0:
            out_ref[z] = q_ref[...]
            iout_ref[z] = i_ref[...]
    for (way, step, part), done in started.items():
        if way == 0 and step == NZ // 2 - 1:
            done.wait_recv()
        done.wait_send()


def gather_line(rows, ints):
    return pl.pallas_call(
        line_gather,
        out_shape=(
            jax.ShapeDtypeStruct((NZ,) + rows.shape, rows.dtype),
            jax.ShapeDtypeStruct((NZ,) + ints.shape, ints.dtype),
        ),
        in_specs=[VM, VM],
        out_specs=(VM, VM),
        scratch_shapes=[
            pltpu.SemaphoreType.DMA((2, NZ // 2, 3)),
            pltpu.SemaphoreType.DMA((2, NZ // 2, 3)),
        ],
        compiler_params=pltpu.CompilerParams(collective_id=0, has_side_effects=True),
    )(rows, ints)


def exchange_kernel(q_ref, s_ref, out_ref, sout_ref, send_sem, recv_sem, ssend, srecv):
    _, me = plane_peer(0)
    greet(plane_peer, NO)
    pl.semaphore_wait(pltpu.get_barrier_semaphore(), NO - 1)

    def copies(k):
        device, place = plane_peer(k)
        return (
            remote(q_ref.at[place], out_ref.at[me], send_sem.at[k], recv_sem.at[k], device),
            remote(s_ref.at[place], sout_ref.at[me], ssend.at[k], srecv.at[k], device),
        )

    @pl.loop(1, NO)
    def _(k):
        for each in copies(k):
            each.start()

    out_ref[me] = q_ref[me]
    sout_ref[me] = s_ref[me]

    @pl.loop(1, NO)
    def _(k):
        for each in copies(k):
            each.wait()


def exchange(rows, slots):
    return pl.pallas_call(
        exchange_kernel,
        out_shape=(
            jax.ShapeDtypeStruct(rows.shape, rows.dtype),
            jax.ShapeDtypeStruct(slots.shape, slots.dtype),
        ),
        in_specs=[VM, VM],
        out_specs=(VM, VM),
        scratch_shapes=[pltpu.SemaphoreType.DMA((NO,)) for _ in range(4)],
        compiler_params=pltpu.CompilerParams(collective_id=1, has_side_effects=True),
    )(rows, slots)


def token_kernel(
    picks_ref, embed_ref, w_ref, ws_ref, out_ref,
    p1, r1, s2, r2, s3, r3, r4, rows, gu, r5,
    ss1, rs1, ss2, rs2, ss3, rs3, ss4, rs4, ss5, rs5,
):
    ns = NX * NC
    _, me = side_peer(0)
    _, z, _, y = here()
    greet(side_peer, ns)
    greet(line_peer, NZ)
    greet(row_peer, NY)
    pl.semaphore_wait(pltpu.get_barrier_semaphore(), ns + NZ + NY - 3)

    def partial(place):
        part = jnp.dot(picks_ref[place], embed_ref[...], preferred_element_type=F32).astype(BF)
        for f in range(8):
            for h in range(2):
                p1[place, 2 * f + h] = part[h * 32 : h * 32 + 32, f * 128 : f * 128 + 128]

    def first(k):
        device, place = side_peer(k)
        return remote(p1.at[place], r1.at[me], ss1.at[k], rs1.at[k], device)

    @pl.loop(1, ns)
    def _(k):
        _, place = side_peer(k)
        partial(place)
        first(k).start()

    partial(me)
    r1[me] = p1[me]

    @pl.loop(1, ns)
    def _(k):
        first(k).wait()

    total = r1[0]
    for j in range(1, ns):
        total = total + r1[j]
    s2[...] = total

    def second(k):
        device, place = line_peer(k)
        return remote(s2.at[place], r2.at[z], ss2.at[k], rs2.at[k], device)

    @pl.loop(1, NZ)
    def _(k):
        second(k).start()

    r2[z] = s2[z]

    @pl.loop(1, NZ)
    def _(k):
        second(k).wait()

    total = r2[0]
    for j in range(1, NZ):
        total = total + r2[j]
    s3[...] = total

    def third(k):
        device, place = line_peer(k)
        return remote(s3, r3.at[z], ss3.at[k], rs3.at[k], device)

    @pl.loop(1, NZ)
    def _(k):
        third(k).start()

    r3[z] = s3[...]

    @pl.loop(1, NZ)
    def _(k):
        third(k).wait()

    def fourth(k):
        device, place = side_peer(k)
        return remote(r3, r4.at[me], ss4.at[k], rs4.at[k], device)

    @pl.loop(1, ns)
    def _(k):
        fourth(k).start()

    r4[me] = r3[...]

    @pl.loop(1, ns)
    def _(k):
        fourth(k).wait()

    for j in range(ns):
        for f in range(8):
            for h in range(2):
                at = j * 64 + h * 32
                rows[at : at + 32, f * 128 : f * 128 + 128] = r4[j, 2 * f + h]

    def fifth(k):
        device, place = row_peer(k)
        return remote(gu.at[place], r5.at[y], ss5.at[k], rs5.at[k], device)

    def project(place):
        block = rows[pl.ds(pl.multiple_of(place * 128, 128), 128), :]
        gu[place] = jnp.dot(block, w_ref[...], preferred_element_type=F32)

    @pl.loop(1, NY)
    def _(k):
        _, place = row_peer(k)
        project(place)
        fifth(k).start()

    project(y)
    r5[y] = gu[y]

    @pl.loop(1, NY)
    def _(k):
        fifth(k).wait()

    both = (r5[0] + r5[1]) + (r5[2] + r5[3])
    gate, up = both[:, :128], both[:, 128:]
    mixed = gate / (1.0 + jnp.exp(-gate)) * up
    score = lax.dot_general(
        ws_ref[...],
        mixed,
        (((1,), (1,)), ((), ())),
        precision=lax.Precision.HIGHEST,
        preferred_element_type=F32,
    )
    out_ref[...] = score


def token_part(picks, embed, w, ws):
    ns = NX * NC
    dma = pltpu.SemaphoreType.DMA
    return pl.pallas_call(
        token_kernel,
        out_shape=jax.ShapeDtypeStruct((8, 128), F32),
        in_specs=[VM] * 4,
        out_specs=VM,
        scratch_shapes=[
            pltpu.VMEM((ns, NZ, 32, 128), BF),
            pltpu.VMEM((ns, NZ, 32, 128), BF),
            pltpu.VMEM((NZ, 32, 128), BF),
            pltpu.VMEM((NZ, 32, 128), BF),
            pltpu.VMEM((32, 128), BF),
            pltpu.VMEM((NZ, 32, 128), BF),
            pltpu.VMEM((ns, NZ, 32, 128), BF),
            pltpu.VMEM((512, 1024), BF),
            pltpu.VMEM((NY, 128, 256), F32),
            pltpu.VMEM((NY, 128, 256), F32),
            dma((ns,)), dma((ns,)), dma((NZ,)), dma((NZ,)), dma((NZ,)),
            dma((NZ,)), dma((ns,)), dma((ns,)), dma((NY,)), dma((NY,)),
        ],
        compiler_params=pltpu.CompilerParams(collective_id=2, has_side_effects=True),
    )(picks, embed, w, ws)


def return_kernel(
    ret_ref, score_ref, table_ref, out_ref, r1, s2, c1, d2, c2,
    ss1, rs1, cs1, cr1, ss2, rs2, cs2, cr2,
):
    ns = NX * NC
    _, me = plane_peer(0)
    _, side = side_peer(0)
    _, z, _, _ = here()
    greet(plane_peer, NO)
    greet(line_peer, NZ)
    pl.semaphore_wait(pltpu.get_barrier_semaphore(), NO + NZ - 2)

    def back(k):
        device, place = plane_peer(k)
        return remote(ret_ref.at[place], r1.at[me], ss1.at[k], rs1.at[k], device)

    def score1(k):
        device, _ = side_peer(k)
        return remote(score_ref, c1.at[side], cs1.at[k], cr1.at[k], device)

    @pl.loop(1, NO)
    def _(k):
        back(k).start()

    @pl.loop(1, ns)
    def _(k):
        score1(k).start()

    r1[me] = ret_ref[me]
    c1[side] = score_ref[...]

    @pl.loop(1, NO)
    def _(k):
        back(k).wait()

    @pl.loop(1, ns)
    def _(k):
        score1(k).wait()

    total = r1[0]
    for j in range(1, NO):
        total = total + r1[j]
    s2[...] = total
    total = c1[0]
    for j in range(1, ns):
        total = total + c1[j]
    d2[...] = total

    def line(k):
        device, place = line_peer(k)
        return (
            remote(s2.at[place], table_ref.at[z], ss2.at[k], rs2.at[k], device),
            remote(d2, c2.at[z], cs2.at[k], cr2.at[k], device),
        )

    @pl.loop(1, NZ)
    def _(k):
        for each in line(k):
            each.start()

    table_ref[z] = s2[z]
    c2[z] = d2[...]

    @pl.loop(1, NZ)
    def _(k):
        for each in line(k):
            each.wait()

    total = c2[0]
    for j in range(1, NZ):
        total = total + c2[j]
    out_ref[...] = total


def give_back(ret, score):
    ns = NX * NC
    dma = pltpu.SemaphoreType.DMA
    return pl.pallas_call(
        return_kernel,
        out_shape=(
            jax.ShapeDtypeStruct((NZ, 1, 128), F32),
            jax.ShapeDtypeStruct((1, 128), F32),
        ),
        in_specs=[VM, VM],
        out_specs=(VM, VM),
        scratch_shapes=[
            pltpu.VMEM((NO, NZ, 1, 128), F32),
            pltpu.VMEM((NZ, 1, 128), F32),
            pltpu.VMEM((ns, 1, 128), F32),
            pltpu.VMEM((1, 128), F32),
            pltpu.VMEM((NZ, 1, 128), F32),
            dma((NO,)), dma((NO,)), dma((ns,)), dma((ns,)),
            dma((NZ,)), dma((NZ,)), dma((NZ,)), dma((NZ,)),
        ],
        compiler_params=pltpu.CompilerParams(collective_id=3, has_side_effects=True),
    )(ret, score)


def body(
    queries,
    class_in,
    class_out,
    passages,
    bucket_sizes,
    bucket_owner,
    bucket_slot,
    embed,
    w_gate,
    w_up,
    w_score,
    block_tokens,
):
    x, z, c, y = here()
    mine = (x * NC + c) * NY + y
    rows, top = bucket_owner.shape
    width = queries.shape[1]
    i32 = jnp.int32

    owner_flat = bucket_owner.reshape(rows * top)
    order = jnp.arange(rows * top, dtype=i32)
    earlier = (owner_flat[:, None] == owner_flat[None, :]) & (order[None, :] < order[:, None])
    rank = jnp.sum(earlier.astype(i32), axis=1).reshape(rows, top)
    own_y = bucket_owner % NY
    own_c = (bucket_owner // NY) % NC
    own_z = (bucket_owner // (NY * NC)) % NZ
    own_x = bucket_owner // (NY * NC * NZ)
    own_o = (own_x * NC + own_c) * NY + own_y
    code = (own_z * NO + own_o) * 2 + rank
    ints = jnp.concatenate([code.T, bucket_slot.T + 1], axis=0)
    ints = jnp.pad(ints, ((0, 0), (0, 128 - rows)))

    line_rows, line_ints = gather_line(queries.reshape(2, rows // 2, width), ints)
    line_rows = line_rows.reshape(NZ * rows, width)
    line_code = line_ints[:, :top, :rows].transpose(1, 0, 2).reshape(top, NZ * rows)
    line_slot = line_ints[:, top : 2 * top, :rows].transpose(1, 0, 2).reshape(top, NZ * rows)
    wanted = z * NO + jnp.arange(NO, dtype=i32)
    hit = (line_code // 2)[None, :, :] == wanted[:, None, None]
    turn = jnp.sum(jnp.where(hit, line_code[None] % 2 + 1, 0), axis=1)
    slot_of = jnp.sum(jnp.where(hit, line_slot[None], 0), axis=1)
    place = jnp.arange(NZ * 2, dtype=i32)
    col = jnp.arange(NZ * rows, dtype=i32)
    chosen = (turn[:, None, :] == (place % 2 + 1)[None, :, None]) & (
        (place // 2)[:, None] == (col // rows)[None, :]
    )[None]
    send_slots = jnp.sum(jnp.where(chosen, slot_of[:, None, :], 0), axis=2)
    send_rows = jnp.dot(
        chosen.astype(BF).reshape(NO * NZ * 2, NZ * rows), line_rows, preferred_element_type=F32
    ).astype(BF)
    send_slots = jnp.pad(send_slots, ((0, 0), (0, 128 - 2 * NZ))).reshape(NO, 1, 128)
    got_rows, got_slots = exchange(send_rows.reshape(NO, NZ * 2, width), send_slots)
    got_rows = got_rows.reshape(NO * NZ * 2, width)
    got_slots = got_slots.reshape(NO, 128)[:, : 2 * NZ].reshape(NO * NZ * 2) - 1

    hidden = jax.nn.relu(jnp.dot(got_rows, class_in, preferred_element_type=F32)).astype(BF)
    all_logits = jnp.dot(hidden, class_out, preferred_element_type=F32)
    columns = jnp.arange(class_out.shape[1], dtype=i32)
    slot_logit = jnp.sum(jnp.where(got_slots[:, None] == columns[None, :], all_logits, 0.0), axis=1)
    bucket_end = jnp.cumsum(bucket_sizes.reshape(-1))
    positions = jnp.arange(passages.shape[0], dtype=i32)
    passage_bucket = jnp.sum((bucket_end[:, None] <= positions[None, :]).astype(i32), axis=0)
    similar = jnp.einsum("sd,pd->sp", got_rows, passages, preferred_element_type=F32)
    slot_mass = jnp.sum(
        jnp.where(got_slots[:, None] == passage_bucket[None, :], jnp.exp(similar), 0.0), axis=1
    )
    lane = jnp.arange(128, dtype=i32)
    logit3 = slot_logit.reshape(NO, NZ, 2)
    mass3 = slot_mass.reshape(NO, NZ, 2)
    odd = lane % 2 == 1
    spread = jnp.where(
        lane < 64,
        jnp.where(odd, logit3[:, :, 1:], logit3[:, :, :1]),
        jnp.where(odd, mass3[:, :, 1:], mass3[:, :, :1]),
    )
    ret = jnp.where((lane % 64) // 2 == mine, spread, 0.0).reshape(NO, NZ, 1, 128)

    vocab_rows = embed.shape[0]
    local_ids = block_tokens.reshape(-1) - ((x * NZ + z) * NC + c) * vocab_rows
    picks = (local_ids[:, None] == jnp.arange(vocab_rows, dtype=i32)[None, :]).astype(BF)
    fill = 128 - w_gate.shape[1]
    w = jnp.concatenate(
        [jnp.pad(w_gate, ((0, 0), (0, fill))), jnp.pad(w_up, ((0, 0), (0, fill)))], axis=1
    )
    ws = jnp.broadcast_to(jnp.pad(w_score.astype(F32), (0, fill))[None, :], (8, 128))
    score = token_part(picks.reshape(NX * NC, 64, vocab_rows), embed, w, ws)

    table, token_scores = give_back(ret, score[:1])
    table = table.reshape(NZ, 128)
    logit_table = table[:, :64].reshape(NZ * 64)
    mass_table = table[:, 64:].reshape(NZ * 64)
    pick = code.reshape(-1)[:, None] == jnp.arange(NZ * 64, dtype=i32)[None, :]
    bucket_logit = jnp.sum(jnp.where(pick, logit_table[None], 0.0), axis=1).reshape(rows, top)
    bucket_mass = jnp.sum(jnp.where(pick, mass_table[None], 0.0), axis=1).reshape(rows, top)
    return (bucket_logit, bucket_mass, token_scores)


def solution(mesh):
    fine = Mesh(mesh.devices.reshape(NX, NZ, NC, NY), AXES)
    group = ("x", "z", "c")
    placed = (
        P(AXES, None),
        P(),
        P(None, AXES),
        P(AXES, None),
        P(AXES, None),
        P(AXES, None),
        P(AXES, None),
        P(group, "y"),
        P("y", group),
        P("y", group),
        P(group),
        P(),
    )
    return jax.shard_map(
        body,
        mesh=fine,
        in_specs=placed,
        out_specs=(P(AXES, None), P(AXES, None), P("y", None)),
        check_vma=False,
    )
```

time: 1150 us -> 201 us (0.17)
  blocking collectives: 755 us -> 0 us
  waiting for transfers between devices: 213 us -> 0 us
  Pallas kernels: 0 us -> 166 us
  starting transfers between devices: 80.2 us -> 0 us
  local copies, waits for them, and re-layouts: 47.2 us -> 11.5 us
  between operations: 14.6 us -> 0.95 us
    psum x2 -> x0, blocking collectives: 755 us -> none  [the longest x1 505 us: body(): token_rows = lax.psum(partial_rows, 'bucket').astype(jnp.bfloat16)]
    all_to_all x10 -> x0, waiting for transfers between devices: 193 us -> none  [the longest x1 86.8 us: body(): lax.all_to_all(send_hidden, 'bucket', split_axis=0, concat_axis=0, tiled=...]
    pallas_call x0 -> x4, Pallas kernels: none -> 166 us  [the longest x1 67.2 us: token_part(): pl.pallas_call(token_kernel, out_shape=jax.ShapeDtypeStruct((8, 128), F32...]
    all_to_all x10 -> x0, starting transfers between devices: 80.1 us -> none  [the longest x1 20.4 us: body(): lax.all_to_all(send_slots, 'bucket', split_axis=0, concat_axis=0, tiled=T...]
    psum x1 -> x0, waiting for transfers between devices: 20.2 us -> none  [body(): gate_all, up_all = lax.psum((gate_part, up_part), 'rerank')]
    reshape x15 -> x7, local copies, waits for them, and re-layouts: 19.7 us -> 0.8 us  [the longest x1 0.2 us: body(): mass3 = slot_mass.reshape(NO, NZ, 2)]
    all_to_all x10 -> x0, local copies, waits for them, and re-layouts: 16.8 us -> none  [the longest x1 5.33 us: body(): lax.all_to_all(lax.all_to_all(send_hidden, 'bucket', split_axis=0, concat...]
    scatter x2 -> x0, other arithmetic: 15 us -> none  [the longest x1 7.76 us: body(): send_hidden = jnp.zeros((total_slots, hidden_width), jnp.bfloat16).at[tar...]
  transfers between devices with their start and end apart: 11 -> 0, of which waited for: 8 -> 0; matrix products, arithmetic and copies ran while one was open for 6% -> 0% of each run, Pallas kernels for 0% -> 0%
where the time goes in v1:
time: 201 us; the launch traced here: 200 us
  Pallas kernels  166 us (83%)
  local copies, waits for them, and re-layouts  11.5 us (6%)
  other arithmetic  11.3 us (6%)
  matrix products  10.5 us (5%)
    pallas_call x1, Pallas kernels, token_part(): pl.pallas_call(token_kernel, out_shape=jax.ShapeDtypeStruct((8, 128), F32...  67.2 us
    pallas_call x1, Pallas kernels, exchange(): pl.pallas_call(exchange_kernel, out_shape=(jax.ShapeDtypeStruct(rows.shap...  37.7 us
    pallas_call x1, Pallas kernels, gather_line(): pl.pallas_call(line_gather, out_shape=(jax.ShapeDtypeStruct((NZ,) + rows....  37.4 us
    pallas_call x1, Pallas kernels, give_back(): pl.pallas_call(return_kernel, out_shape=(jax.ShapeDtypeStruct((NZ, 1, 128...  23.4 us
    dot_general x1, matrix products, body(): all_logits = jnp.dot(hidden, class_out, preferred_element_type=F32)  4.6 us

profile of v1, /device:TPU:1, one launch (start us, length us, event | category | flops | bytes accessed | tf_op | source)
XLA Modules:
  0.0 199.9 jit_solution(15897311565057793142)
XLA Ops:
  0.6 0.9 copy.43
  1.6 0.3 convert_reduce_fusion.1
  2.0 0.7 fusion.15
  2.8 0.7 add_bitcast_fusion
  3.5 0.6 pad.22.i_ref
  4.1 37.4 %shard_map.139 = (bf16[16,2,32,768]{3,2,1,0:T(8,128)(2,1)}, s32[16,16,128]{2,1,0:T(8,128)}) custom-call(bf16[2,32,768]{2,1,0:T(8,128)(2,1)} %bitcast.35, s32[16,128]{1,0:T(8,128)} %pad.22.i_ref), custom_call_target="tpu_custom_call" | custom-call | tf_op jit(solution)/shard_map/pallas_call | solution.py:109
  41.5 1.0 slice_bitcast_fusion.1
  42.8 0.7 fusion.1
  43.6 1.1 select_reduce_fusion
  44.7 0.6 pad.23
  45.3 0.8 compare_and_fusion
  46.1 3.0 %convolution_convert_fusion = bf16[1024,768]{1,0:T(8,128)(2,1)} fusion(pred[1024,1024]{1,0:T(32,128)(4,1)S(1)} %bitcast.34, bf16[1024,768]{1,0:T(8,128)(2,1)S(1)} %bitcast.45), kind=kOutput, calls=%fused_computation.9 | convolution fusion | flops 1611399168 | bytes 4194304 | tf_op jit(solution)/shard_map/dot_general | solution.py:464
  49.0 37.7 %shard_map.140 = (bf16[32,32,768]{2,1,0:T(8,128)(2,1)}, s32[32,1,128]{2,1,0:T(1,128)}) custom-call(bf16[32,32,768]{2,1,0:T(8,128)(2,1)} %bitcast.33, s32[32,1,128]{2,1,0:T(1,128)} %bitcast.36), custom_call_target="tpu_custom_call" | custom-call | tf_op jit(solution)/shard_map/pallas_call | solution.py:152
  86.7 0.7 slice_add_fusion
  87.5 0.3 reduce-window.9
  88.4 2.9 %select_reduce_fusion.1 = f32[1024]{0:T(1024)S(1)} fusion(bf16[1024,768]{1,0:T(8,128)(2,1)} %bitcast.46, bf16[768,768]{1,0:T(8,128)(2,1)S(1)} %copy-done.6, s32[1024]{0:T(1024)S(1)} %sub.65, s32[768]{0:T(1024)S(1)} %convert_reduce_fusion), kind=kOutput, calls=%fused_computation.3 | convolution fusion | flops 1210317824 | bytes 2763776 | tf_op jit(solution)/shard_map/sd,pd->sp/dot_general | solution.py:479
  91.6 0.2 copy.62
  91.9 0.3 copy.63
  92.1 4.6 %select_reduce_fusion.4 = f32[1024]{0:T(1024)S(1)} fusion(bf16[1024,512]{1,0:T(8,128)(2,1)} %param.14, s32[1024]{0:T(1024)S(1)} %sub.65, bf16[1024,768]{1,0:T(8,128)(2,1)} %bitcast.47, bf16[768,1024]{1,0:T(8,128)(2,1)S(1)} %copy-done), kind=kOutput, calls=%fused_computation.6 | convolution fusion | flops 2688023552 | bytes 4202496 | tf_op jit(solution)/shard_map/dot_general | solution.py:473
  97.4 0.3 copy.61
  97.7 3.1 %broadcast_select_fusion.3.ret_ref = f32[32,16,1,128]{3,2,1,0:T(1,128)} fusion(pred[128]{0:T(512)(128)(4,1)S(1)} %fusion.30, pred[128]{0:T(512)(128)(4,1)S(1)} %get-tuple-element.39, pred[128]{0:T(512)(128)(4,1)S(1)} %get-tuple-element.38, f32[32,16]{1,0:T(8,128)S(1)} %bitcast.38, f32[32,16]{1,0:T(8,128)S(1)} %bitcast.37, f32[32,16]{1,0:T(8,128)S(1)} %bitcast.40, ...), kind=kLoop, calls=%fused_computation.29 | loop fusion | flops 262144 | bytes 270720 | tf_op jit(solution)/shard_map/jit(_where)/select_n | solution.py:492
  100.9 0.9 fusion.6.picks_ref
  102.1 0.9 fusion.5.w_ref
  103.0 0.6 broadcast_in_dim.160.ws_ref
  103.6 67.2 %shard_map.141 = f32[8,128]{1,0:T(8,128)} custom-call(bf16[8,64,256]{2,1,0:T(8,128)(2,1)} %fusion.6.picks_ref, bf16[256,1024]{1,0:T(8,128)(2,1)} %embed_ref.1, bf16[1024,256]{1,0:T(8,128)(2,1)} %fusion.5.w_ref, f32[8,128]{1,0:T(8,128)} %broadcast_in_dim.160.ws_ref), custom_call_target="tpu_custom_call" | custom-call | tf_op jit(solution)/shard_map/pallas_call | solution.py:296
  170.8 1.2 slice.46.score_ref
  172.0 23.4 %shard_map.142 = (f32[16,1,128]{2,1,0:T(1,128)}, f32[1,128]{1,0:T(1,128)}) custom-call(f32[32,16,1,128]{3,2,1,0:T(1,128)} %broadcast_select_fusion.3.ret_ref, f32[1,128]{1,0:T(1,128)} %slice.46.score_ref), custom_call_target="tpu_custom_call" | custom-call | tf_op jit(solution)/shard_map/pallas_call | solution.py:396
  195.4 0.8 fusion.34
  196.6 0.7 select_reduce_fusion.2
  197.4 0.7 copy.58
  198.1 0.7 copy.59
  198.8 1.1 copy.67
  (54 shorter events, 3.1 us)
Async XLA Ops:
  0.6 91.5 %copy-start = (bf16[768,1024]{1,0:T(8,128)(2,1)S(1)}, bf16[768,1024]{1,0:T(8,128)(2,1)}, u32[]{:S(2)}) copy-start(bf16[768,1024]{1,0:T(8,128)(2,1)} %param.13) | copy-start | bytes 4718596
  41.5 4.6 %copy-start.5 = (bf16[16,2,32,768]{3,2,1,0:T(8,128)(2,1)S(1)}, bf16[16,2,32,768]{3,2,1,0:T(8,128)(2,1)}, u32[]{:S(2)}) copy-start(bf16[16,2,32,768]{3,2,1,0:T(8,128)(2,1)} %get-tuple-element.10) | copy-start | bytes 4718596
  49.0 38.5 %copy-start.3 = (s32[1,512]{1,0:T(1,128)S(1)}, s32[1,512]{1,0:T(1,128)}, u32[]{:S(2)}) copy-start(s32[1,512]{1,0:T(1,128)} %param.16) | copy-start | bytes 6148
  49.0 39.3 %copy-start.6 = (bf16[768,768]{1,0:T(8,128)(2,1)S(1)}, bf16[768,768]{1,0:T(8,128)(2,1)}, u32[]{:S(2)}) copy-start(bf16[768,768]{1,0:T(8,128)(2,1)} %param.15) | copy-start | bytes 3538948
  96.8 4.0 %copy-start.4 = (s32[4,128]{1,0:T(4,128)S(1)}, s32[4,128]{1,0:T(4,128)}, u32[]{:S(2)}) copy-start(s32[4,128]{1,0:T(4,128)} %param.23) | copy-start | bytes 6148
  96.8 5.0 %copy-start.1 = (bf16[1024,112]{0,1:T(8,128)(2,1)S(1)}, bf16[1024,112]{0,1:T(8,128)(2,1)}, u32[]{:S(2)}) copy-start(bf16[1024,112]{0,1:T(8,128)(2,1)} %param.20) | copy-start | bytes 688132
  96.8 5.1 %copy-start.2 = (bf16[1024,112]{0,1:T(8,128)(2,1)S(1)}, bf16[1024,112]{0,1:T(8,128)(2,1)}, u32[]{:S(2)}) copy-start(bf16[1024,112]{0,1:T(8,128)(2,1)} %param.21) | copy-start | bytes 688132
  97.1 5.8 %copy-start.7 = (bf16[112]{0:T(256)(128)(2,1)S(1)}, bf16[112]{0:T(256)(128)(2,1)}, u32[]{:S(2)}) copy-start(bf16[112]{0:T(256)(128)(2,1)} %param.22) | copy-start | bytes 676

commit v2 on v1

--- a/solution.py
+++ b/solution.py
@@ -1,5 +1,3 @@
-import functools
-
 import jax
 import jax.numpy as jnp
 from jax import lax
@@ -66,14 +64,18 @@
     return (x, z, c, py), py
 
 
-def line_gather(q_ref, i_ref, out_ref, iout_ref, send_sem, recv_sem):
-    x, z, c, y = here()
+def line_kernel(
+    q_ref, i_ref, picks_ref, embed_ref, out_ref, iout_ref, r3_ref,
+    p1, r1, s2, r2, s3, send_sem, recv_sem, ss1, rs1, ss2, rs2, ss3, rs3,
+):
+    ns = NX * NC
+    x, z, c, y = here()
+    _, me = side_peer(0)
     right = (x, lax.rem(z + 1, NZ), c, y)
     left = (x, lax.rem(z + NZ - 1, NZ), c, y)
-    barrier = pltpu.get_barrier_semaphore()
-    for device in (left, right):
-        pl.semaphore_signal(barrier, inc=1, device_id=device, device_id_type=pl.DeviceIdType.MESH)
-    pl.semaphore_wait(barrier, 2)
+    greet(line_peer, NZ)
+    greet(side_peer, ns)
+    pl.semaphore_wait(pltpu.get_barrier_semaphore(), NZ + ns - 2)
 
     def copy(way, step, part):
         place = lax.rem(z + (NZ - step if way == 0 else step), NZ)
@@ -86,6 +88,56 @@
             dst = iout_ref.at[place]
         return remote(src, dst, send_sem.at[way, step, part], recv_sem.at[way, step, part], device)
 
+    def partial(place):
+        part = jnp.dot(picks_ref[place], embed_ref[...], preferred_element_type=F32).astype(BF)
+        for f in range(8):
+            for h in range(2):
+                p1[place, 2 * f + h] = part[h * 32 : h * 32 + 32, f * 128 : f * 128 + 128]
+
+    def first(k):
+        device, place = side_peer(k)
+        return remote(p1.at[place], r1.at[me], ss1.at[k], rs1.at[k], device)
+
+    def second(k):
+        device, place = line_peer(k)
+        return remote(s2.at[place], r2.at[z], ss2.at[k], rs2.at[k], device)
+
+    def third(k):
+        device, _ = line_peer(k)
+        return remote(s3, r3_ref.at[z], ss3.at[k], rs3.at[k], device)
+
+    def start_second():
+        @pl.loop(1, ns)
+        def _(k):
+            first(k).wait()
+
+        total = r1[0]
+        for j in range(1, ns):
+            total = total + r1[j]
+        s2[...] = total
+
+        @pl.loop(1, NZ)
+        def _(k):
+            second(k).start()
+
+        r2[z] = s2[z]
+
+    def start_third():
+        @pl.loop(1, NZ)
+        def _(k):
+            second(k).wait()
+
+        total = r2[0]
+        for j in range(1, NZ):
+            total = total + r2[j]
+        s3[...] = total
+
+        @pl.loop(1, NZ)
+        def _(k):
+            third(k).start()
+
+        r3_ref[z] = s3[...]
+
     started = {}
     for step in range(NZ // 2):
         for part in (2, 0, 1):
@@ -96,36 +148,75 @@
                     continue
                 started[way, step, part] = copy(way, step, part)
                 started[way, step, part].start()
-        if step == 0:
+        if step < 4:
+
+            @pl.loop(1 + 2 * step, min(3 + 2 * step, ns))
+            def _(k):
+                _, place = side_peer(k)
+                partial(place)
+                first(k).start()
+
+        if step == 3:
+            partial(me)
+            r1[me] = p1[me]
             out_ref[z] = q_ref[...]
             iout_ref[z] = i_ref[...]
+        if step == 5:
+            start_second()
+    start_third()
     for (way, step, part), done in started.items():
         if way == 0 and step == NZ // 2 - 1:
             done.wait_recv()
         done.wait_send()
 
-
-def gather_line(rows, ints):
+    @pl.loop(1, NZ)
+    def _(k):
+        third(k).wait()
+
+
+def gather_line(rows, ints, picks, embed):
+    ns = NX * NC
+    dma = pltpu.SemaphoreType.DMA
     return pl.pallas_call(
-        line_gather,
+        line_kernel,
         out_shape=(
             jax.ShapeDtypeStruct((NZ,) + rows.shape, rows.dtype),
             jax.ShapeDtypeStruct((NZ,) + ints.shape, ints.dtype),
+            jax.ShapeDtypeStruct((NZ, 32, 128), BF),
         ),
-        in_specs=[VM, VM],
-        out_specs=(VM, VM),
+        in_specs=[VM] * 4,
+        out_specs=(VM, VM, VM),
         scratch_shapes=[
-            pltpu.SemaphoreType.DMA((2, NZ // 2, 3)),
-            pltpu.SemaphoreType.DMA((2, NZ // 2, 3)),
+            pltpu.VMEM((ns, NZ, 32, 128), BF),
+            pltpu.VMEM((ns, NZ, 32, 128), BF),
+            pltpu.VMEM((NZ, 32, 128), BF),
+            pltpu.VMEM((NZ, 32, 128), BF),
+            pltpu.VMEM((32, 128), BF),
+            dma((2, NZ // 2, 3)), dma((2, NZ // 2, 3)),
+            dma((ns,)), dma((ns,)), dma((NZ,)), dma((NZ,)), dma((NZ,)), dma((NZ,)),
         ],
         compiler_params=pltpu.CompilerParams(collective_id=0, has_side_effects=True),
-    )(rows, ints)
-
-
-def exchange_kernel(q_ref, s_ref, out_ref, sout_ref, send_sem, recv_sem, ssend, srecv):
+    )(rows, ints, picks, embed)
+
+
+def exchange_kernel(
+    q_ref, s_ref, r3_ref, w_ref, ws_ref, out_ref, sout_ref, score_ref,
+    r4, rows, gu, r5, send_sem, recv_sem, ssend, srecv, ss4, rs4, sc4, rc4, ss5, rs5,
+):
+    x, z, c, y = here()
+    ns = NX * NC
     _, me = plane_peer(0)
     greet(plane_peer, NO)
     pl.semaphore_wait(pltpu.get_barrier_semaphore(), NO - 1)
+    partner = (x, z, 1 - c, y)
+
+    def along_x(k):
+        device = (lax.rem(x + k, NX), z, c, y)
+        return remote(r3_ref, r4.at[x * NC + c], ss4.at[k], rs4.at[k], device)
+
+    def across(k):
+        place = lax.rem(x + NX - k, NX) * NC + c
+        return remote(r4.at[place], r4.at[place], sc4.at[k], rc4.at[k], partner)
 
     def copies(k):
         device, place = plane_peer(k)
@@ -134,6 +225,11 @@
             remote(s_ref.at[place], sout_ref.at[me], ssend.at[k], srecv.at[k], device),
         )
 
+    for k in (2, 1, 3):
+        along_x(k).start()
+    r4[x * NC + c] = r3_ref[...]
+    across(0).start()
+
     @pl.loop(1, NO)
     def _(k):
         for each in copies(k):
@@ -142,178 +238,83 @@
     out_ref[me] = q_ref[me]
     sout_ref[me] = s_ref[me]
 
+    for k in (1, 3, 2):
+        along_x(k).wait_recv()
+        across(k).start()
+    for k in range(NX):
+        across(k).wait_recv()
+
+    for j in range(ns):
+        for f in range(8):
+            for h in range(2):
+                at = j * 64 + h * 32
+                rows[at : at + 32, f * 128 : f * 128 + 128] = r4[j, 2 * f + h]
+
+    def fifth(k):
+        device, place = row_peer(k)
+        return remote(gu.at[place], r5.at[y], ss5.at[k], rs5.at[k], device)
+
+    def project(place):
+        block = rows[pl.ds(pl.multiple_of(place * 128, 128), 128), :]
+        gu[place] = jnp.dot(block, w_ref[...], preferred_element_type=F32)
+
+    @pl.loop(1, NY)
+    def _(k):
+        _, place = row_peer(k)
+        project(place)
+        fifth(k).start()
+
+    project(y)
+    r5[y] = gu[y]
+
     @pl.loop(1, NO)
     def _(k):
         for each in copies(k):
             each.wait()
 
-
-def exchange(rows, slots):
+    @pl.loop(1, NY)
+    def _(k):
+        fifth(k).wait()
+
+    for k in range(1, NX):
+        along_x(k).wait_send()
+    for k in range(NX):
+        across(k).wait_send()
+
+    both = (r5[0] + r5[1]) + (r5[2] + r5[3])
+    gate, up = both[:, :128], both[:, 128:]
+    mixed = gate / (1.0 + jnp.exp(-gate)) * up
+    score_ref[...] = lax.dot_general(
+        ws_ref[...],
+        mixed,
+        (((1,), (1,)), ((), ())),
+        precision=lax.Precision.HIGHEST,
+        preferred_element_type=F32,
+    )
+
+
+def exchange(rows, slots, r3, w, ws):
+    ns = NX * NC
+    dma = pltpu.SemaphoreType.DMA
     return pl.pallas_call(
         exchange_kernel,
         out_shape=(
             jax.ShapeDtypeStruct(rows.shape, rows.dtype),
             jax.ShapeDtypeStruct(slots.shape, slots.dtype),
+            jax.ShapeDtypeStruct((8, 128), F32),
         ),
-        in_specs=[VM, VM],
-        out_specs=(VM, VM),
-        scratch_shapes=[pltpu.SemaphoreType.DMA((NO,)) for _ in range(4)],
-        compiler_params=pltpu.CompilerParams(collective_id=1, has_side_effects=True),
-    )(rows, slots)
-
-
-def token_kernel(
-    picks_ref, embed_ref, w_ref, ws_ref, out_ref,
-    p1, r1, s2, r2, s3, r3, r4, rows, gu, r5,
-    ss1, rs1, ss2, rs2, ss3, rs3, ss4, rs4, ss5, rs5,
-):
-    ns = NX * NC
-    _, me = side_peer(0)
-    _, z, _, y = here()
-    greet(side_peer, ns)
-    greet(line_peer, NZ)
-    greet(row_peer, NY)
-    pl.semaphore_wait(pltpu.get_barrier_semaphore(), ns + NZ + NY - 3)
-
-    def partial(place):
-        part = jnp.dot(picks_ref[place], embed_ref[...], preferred_element_type=F32).astype(BF)
-        for f in range(8):
-            for h in range(2):
-                p1[place, 2 * f + h] = part[h * 32 : h * 32 + 32, f * 128 : f * 128 + 128]
-
-    def first(k):
-        device, place = side_peer(k)
-        return remote(p1.at[place], r1.at[me], ss1.at[k], rs1.at[k], device)
-
-    @pl.loop(1, ns)
-    def _(k):
-        _, place = side_peer(k)
-        partial(place)
-        first(k).start()
-
-    partial(me)
-    r1[me] = p1[me]
-
-    @pl.loop(1, ns)
-    def _(k):
-        first(k).wait()
-
-    total = r1[0]
-    for j in range(1, ns):
-        total = total + r1[j]
-    s2[...] = total
-
-    def second(k):
-        device, place = line_peer(k)
-        return remote(s2.at[place], r2.at[z], ss2.at[k], rs2.at[k], device)
-
-    @pl.loop(1, NZ)
-    def _(k):
-        second(k).start()
-
-    r2[z] = s2[z]
-
-    @pl.loop(1, NZ)
-    def _(k):
-        second(k).wait()
-
-    total = r2[0]
-    for j in range(1, NZ):
-        total = total + r2[j]
-    s3[...] = total
-
-    def third(k):
-        device, place = line_peer(k)
-        return remote(s3, r3.at[z], ss3.at[k], rs3.at[k], device)
-
-    @pl.loop(1, NZ)
-    def _(k):
-        third(k).start()
-
-    r3[z] = s3[...]
-
-    @pl.loop(1, NZ)
-    def _(k):
-        third(k).wait()
-
-    def fourth(k):
-        device, place = side_peer(k)
-        return remote(r3, r4.at[me], ss4.at[k], rs4.at[k], device)
-
-    @pl.loop(1, ns)
-    def _(k):
-        fourth(k).start()
-
-    r4[me] = r3[...]
-
-    @pl.loop(1, ns)
-    def _(k):
-        fourth(k).wait()
-
-    for j in range(ns):
-        for f in range(8):
-            for h in range(2):
-                at = j * 64 + h * 32
-                rows[at : at + 32, f * 128 : f * 128 + 128] = r4[j, 2 * f + h]
-
-    def fifth(k):
-        device, place = row_peer(k)
-        return remote(gu.at[place], r5.at[y], ss5.at[k], rs5.at[k], device)
-
-    def project(place):
-        block = rows[pl.ds(pl.multiple_of(place * 128, 128), 128), :]
-        gu[place] = jnp.dot(block, w_ref[...], preferred_element_type=F32)
-
-    @pl.loop(1, NY)
-    def _(k):
-        _, place = row_peer(k)
-        project(place)
-        fifth(k).start()
-
-    project(y)
-    r5[y] = gu[y]
-
-    @pl.loop(1, NY)
-    def _(k):
-        fifth(k).wait()
-
-    both = (r5[0] + r5[1]) + (r5[2] + r5[3])
-    gate, up = both[:, :128], both[:, 128:]
-    mixed = gate / (1.0 + jnp.exp(-gate)) * up
-    score = lax.dot_general(
-        ws_ref[...],
-        mixed,
-        (((1,), (1,)), ((), ())),
-        precision=lax.Precision.HIGHEST,
-        preferred_element_type=F32,
-    )
-    out_ref[...] = score
-
-
-def token_part(picks, embed, w, ws):
-    ns = NX * NC
-    dma = pltpu.SemaphoreType.DMA
-    return pl.pallas_call(
-        token_kernel,
-        out_shape=jax.ShapeDtypeStruct((8, 128), F32),
-        in_specs=[VM] * 4,
-        out_specs=VM,
+        in_specs=[VM] * 5,
+        out_specs=(VM, VM, VM),
         scratch_shapes=[
-            pltpu.VMEM((ns, NZ, 32, 128), BF),
-            pltpu.VMEM((ns, NZ, 32, 128), BF),
-            pltpu.VMEM((NZ, 32, 128), BF),
-            pltpu.VMEM((NZ, 32, 128), BF),
-            pltpu.VMEM((32, 128), BF),
-            pltpu.VMEM((NZ, 32, 128), BF),
             pltpu.VMEM((ns, NZ, 32, 128), BF),
             pltpu.VMEM((512, 1024), BF),
             pltpu.VMEM((NY, 128, 256), F32),
             pltpu.VMEM((NY, 128, 256), F32),
-            dma((ns,)), dma((ns,)), dma((NZ,)), dma((NZ,)), dma((NZ,)),
-            dma((NZ,)), dma((ns,)), dma((ns,)), dma((NY,)), dma((NY,)),
+            dma((NO,)), dma((NO,)), dma((NO,)), dma((NO,)),
+            dma((NX,)), dma((NX,)), dma((NX,)), dma((NX,)), dma((NY,)), dma((NY,)),
         ],
-        compiler_params=pltpu.CompilerParams(collective_id=2, has_side_effects=True),
-    )(picks, embed, w, ws)
+        compiler_params=pltpu.CompilerParams(collective_id=1, has_side_effects=True),
+    )(rows, slots, r3, w, ws)
 
 
 def return_kernel(
@@ -387,7 +388,7 @@
     total = c2[0]
     for j in range(1, NZ):
         total = total + c2[j]
-    out_ref[...] = total
+    out_ref[...] = total[:1]
 
 
 def give_back(ret, score):
@@ -404,9 +405,9 @@
         scratch_shapes=[
             pltpu.VMEM((NO, NZ, 1, 128), F32),
             pltpu.VMEM((NZ, 1, 128), F32),
-            pltpu.VMEM((ns, 1, 128), F32),
-            pltpu.VMEM((1, 128), F32),
-            pltpu.VMEM((NZ, 1, 128), F32),
+            pltpu.VMEM((ns, 8, 128), F32),
+            pltpu.VMEM((8, 128), F32),
+            pltpu.VMEM((NZ, 8, 128), F32),
             dma((NO,)), dma((NO,)), dma((ns,)), dma((ns,)),
             dma((NZ,)), dma((NZ,)), dma((NZ,)), dma((NZ,)),
         ],
@@ -447,7 +448,17 @@
     ints = jnp.concatenate([code.T, bucket_slot.T + 1], axis=0)
     ints = jnp.pad(ints, ((0, 0), (0, 128 - rows)))
 
-    line_rows, line_ints = gather_line(queries.reshape(2, rows // 2, width), ints)
+    vocab_rows = embed.shape[0]
+    local_ids = block_tokens.reshape(-1) - ((x * NZ + z) * NC + c) * vocab_rows
+    picks = (local_ids[:, None] == jnp.arange(vocab_rows, dtype=i32)[None, :]).astype(BF)
+    fill = 128 - w_gate.shape[1]
+    w = jnp.concatenate(
+        [jnp.pad(w_gate, ((0, 0), (0, fill))), jnp.pad(w_up, ((0, 0), (0, fill)))], axis=1
+    )
+    ws = jnp.broadcast_to(jnp.pad(w_score.astype(F32), (0, fill))[None, :], (8, 128))
+    line_rows, line_ints, line_tokens = gather_line(
+        queries.reshape(2, rows // 2, width), ints, picks.reshape(NX * NC, 64, vocab_rows), embed
+    )
     line_rows = line_rows.reshape(NZ * rows, width)
     line_code = line_ints[:, :top, :rows].transpose(1, 0, 2).reshape(top, NZ * rows)
     line_slot = line_ints[:, top : 2 * top, :rows].transpose(1, 0, 2).reshape(top, NZ * rows)
@@ -465,7 +476,9 @@
         chosen.astype(BF).reshape(NO * NZ * 2, NZ * rows), line_rows, preferred_element_type=F32
     ).astype(BF)
     send_slots = jnp.pad(send_slots, ((0, 0), (0, 128 - 2 * NZ))).reshape(NO, 1, 128)
-    got_rows, got_slots = exchange(send_rows.reshape(NO, NZ * 2, width), send_slots)
+    got_rows, got_slots, score = exchange(
+        send_rows.reshape(NO, NZ * 2, width), send_slots, line_tokens, w, ws
+    )
     got_rows = got_rows.reshape(NO * NZ * 2, width)
     got_slots = got_slots.reshape(NO, 128)[:, : 2 * NZ].reshape(NO * NZ * 2) - 1
 
@@ -491,17 +504,7 @@
     )
     ret = jnp.where((lane % 64) // 2 == mine, spread, 0.0).reshape(NO, NZ, 1, 128)
 
-    vocab_rows = embed.shape[0]
-    local_ids = block_tokens.reshape(-1) - ((x * NZ + z) * NC + c) * vocab_rows
-    picks = (local_ids[:, None] == jnp.arange(vocab_rows, dtype=i32)[None, :]).astype(BF)
-    fill = 128 - w_gate.shape[1]
-    w = jnp.concatenate(
-        [jnp.pad(w_gate, ((0, 0), (0, fill))), jnp.pad(w_up, ((0, 0), (0, fill)))], axis=1
-    )
-    ws = jnp.broadcast_to(jnp.pad(w_score.astype(F32), (0, fill))[None, :], (8, 128))
-    score = token_part(picks.reshape(NX * NC, 64, vocab_rows), embed, w, ws)
-
-    table, token_scores = give_back(ret, score[:1])
+    table, token_scores = give_back(ret, score)
     table = table.reshape(NZ, 128)
     logit_table = table[:, :64].reshape(NZ * 64)
     mass_table = table[:, 64:].reshape(NZ * 64)

time: 201 us -> 158 us (0.79)
  Pallas kernels: 166 us -> 123 us
    pallas_call x2 -> x1, Pallas kernels: 105 us -> 54.8 us  [gather_line(): pl.pallas_call(line_kernel, out_shape=(jax.ShapeDtypeStruct((NZ,) + rows....]
    pallas_call x1, Pallas kernels: 37.7 us -> 43.4 us  [exchange(): pl.pallas_call(exchange_kernel, out_shape=(jax.ShapeDtypeStruct(rows.shap...]
where the time goes in v2:
time: 158 us; the launch traced here: 157 us
  Pallas kernels  123 us (78%)
  other arithmetic  12.1 us (8%)
  matrix products  10.5 us (7%)
  local copies, waits for them, and re-layouts  10 us (6%)
    pallas_call x1, Pallas kernels, gather_line(): pl.pallas_call(line_kernel, out_shape=(jax.ShapeDtypeStruct((NZ,) + rows....  54.8 us
    pallas_call x1, Pallas kernels, exchange(): pl.pallas_call(exchange_kernel, out_shape=(jax.ShapeDtypeStruct(rows.shap...  43.4 us
    pallas_call x1, Pallas kernels, give_back(): pl.pallas_call(return_kernel, out_shape=(jax.ShapeDtypeStruct((NZ, 1, 128...  25.2 us
    dot_general x1, matrix products, body(): all_logits = jnp.dot(hidden, class_out, preferred_element_type=F32)  4.29 us
    unnamed x20, local copies, waits for them, and re-layouts  3.6 us
    dot_general x1, matrix products, body(): jnp.einsum('sd,pd->sp', got_rows, passages, preferred_element_type=F32)  3.24 us

profile of v2, /device:TPU:1, one launch (start us, length us, event | category | flops | bytes accessed | tf_op | source)
XLA Modules:
  0.0 157.0 jit_solution(11519341998343194812)
XLA Ops:
  0.7 0.8 broadcast_subtract_fusion
  1.5 0.8 fusion.6.picks_ref
  2.4 0.8 copy.43
  3.2 0.3 convert_reduce_fusion.1
  3.7 0.7 fusion.15
  4.4 0.7 add_bitcast_fusion
  5.1 0.6 pad.22.i_ref
  5.7 54.8 %shard_map.139 = (bf16[16,2,32,768]{3,2,1,0:T(8,128)(2,1)}, s32[16,16,128]{2,1,0:T(8,128)}, bf16[16,32,128]{2,1,0:T(8,128)(2,1)}) custom-call(bf16[2,32,768]{2,1,0:T(8,128)(2,1)} %bitcast.35, s32[16,128]{1,0:T(8,128)} %pad.22.i_ref, bf16[8,64,256]{2,1,0:T(8,128)(2,1)} %fusion.6.picks_ref, bf16[256,1024]{1,0:T(8,128)(2,1)} %embed_ref.1), custom_call_target="tpu_custom_call" | custom-call | tf_op jit(solution)/shard_map/pallas_call | solution.py:180
  60.5 0.9 slice_bitcast_fusion.1
  61.7 0.7 fusion.1
  62.5 1.1 select_reduce_fusion
  63.6 0.6 pad.23
  64.2 0.8 compare_and_fusion
  65.0 3.0 %convolution_convert_fusion = bf16[1024,768]{1,0:T(8,128)(2,1)} fusion(pred[1024,1024]{1,0:T(32,128)(4,1)S(1)} %bitcast.34, bf16[1024,768]{1,0:T(8,128)(2,1)S(1)} %bitcast.45), kind=kOutput, calls=%fused_computation.9 | convolution fusion | flops 1611399168 | bytes 4194304 | tf_op jit(solution)/shard_map/dot_general | solution.py:475
  68.3 0.9 fusion.5.w_ref
  69.2 0.6 broadcast_in_dim.149.ws_ref
  69.8 43.4 %shard_map.140 = (bf16[32,32,768]{2,1,0:T(8,128)(2,1)}, s32[32,1,128]{2,1,0:T(1,128)}, f32[8,128]{1,0:T(8,128)}) custom-call(bf16[32,32,768]{2,1,0:T(8,128)(2,1)} %bitcast.33, s32[32,1,128]{2,1,0:T(1,128)} %bitcast.36, bf16[16,32,128]{2,1,0:T(8,128)(2,1)} %get-tuple-element.13.r3_ref, bf16[1024,256]{1,0:T(8,128)(2,1)} %fusion.5.w_ref, ...), custom_call_target="tpu_custom_call" | custom-call | tf_op jit(solution)/shard_map/pallas_call | solution.py:299
  113.2 0.7 slice_add_fusion
  114.0 4.3 %select_reduce_fusion.4 = f32[1024]{0:T(1024)S(1)} fusion(bf16[1024,512]{1,0:T(8,128)(2,1)S(1)} %copy-done.5, s32[1024]{0:T(1024)S(1)} %sub.68, bf16[1024,768]{1,0:T(8,128)(2,1)} %bitcast.46, bf16[768,1024]{1,0:T(8,128)(2,1)S(1)} %copy-done), kind=kOutput, calls=%fused_computation.6 | convolution fusion | flops 2688023552 | bytes 4202496 | tf_op jit(solution)/shard_map/dot_general | solution.py:486
  118.6 0.2 copy.60
  118.9 0.3 copy.61
  119.2 0.3 reduce-window.9
  120.0 3.2 %select_reduce_fusion.1 = f32[1024]{0:T(1024)S(1)} fusion(bf16[1024,768]{1,0:T(8,128)(2,1)} %bitcast.47, bf16[768,768]{1,0:T(8,128)(2,1)} %param.15, s32[1024]{0:T(1024)S(1)} %sub.68, s32[768]{0:T(1024)S(1)} %convert_reduce_fusion), kind=kOutput, calls=%fused_computation.3 | convolution fusion | flops 1210317824 | bytes 2763776 | tf_op jit(solution)/shard_map/sd,pd->sp/dot_general | solution.py:492
  123.6 0.2 copy.62
  123.9 0.3 copy.63
  124.2 3.1 %broadcast_select_fusion.3.ret_ref = f32[32,16,1,128]{3,2,1,0:T(1,128)} fusion(pred[128]{0:T(512)(128)(4,1)S(1)} %fusion.30, pred[128]{0:T(512)(128)(4,1)S(1)} %get-tuple-element.43, pred[128]{0:T(512)(128)(4,1)S(1)} %get-tuple-element.42, f32[32,16]{1,0:T(8,128)S(1)} %bitcast.40, f32[32,16]{1,0:T(8,128)S(1)} %bitcast.39, f32[32,16]{1,0:T(8,128)S(1)} %bitcast.38, ...), kind=kLoop, calls=%fused_computation.29 | loop fusion | flops 262144 | bytes 270720 | tf_op jit(solution)/shard_map/jit(_where)/select_n | solution.py:505
  127.3 25.2 %shard_map.141 = (f32[16,1,128]{2,1,0:T(1,128)}, f32[1,128]{1,0:T(1,128)}) custom-call(f32[32,16,1,128]{3,2,1,0:T(1,128)} %broadcast_select_fusion.3.ret_ref, f32[8,128]{1,0:T(8,128)} %get-tuple-element.16.score_ref), custom_call_target="tpu_custom_call" | custom-call | tf_op jit(solution)/shard_map/pallas_call | solution.py:397
  152.5 0.8 fusion.34
  153.6 0.7 select_reduce_fusion.2
  154.5 0.7 copy.58
  155.2 0.7 copy.59
  155.9 1.1 copy.67
  (50 shorter events, 2.8 us)
Async XLA Ops:
  0.6 113.4 %copy-start = (bf16[768,1024]{1,0:T(8,128)(2,1)S(1)}, bf16[768,1024]{1,0:T(8,128)(2,1)}, u32[]{:S(2)}) copy-start(bf16[768,1024]{1,0:T(8,128)(2,1)} %param.13) | copy-start | bytes 4718596
  61.7 3.3 %copy-start.4 = (bf16[16,2,32,768]{3,2,1,0:T(8,128)(2,1)S(1)}, bf16[16,2,32,768]{3,2,1,0:T(8,128)(2,1)}, u32[]{:S(2)}) copy-start(bf16[16,2,32,768]{3,2,1,0:T(8,128)(2,1)} %get-tuple-element.12) | copy-start | bytes 4718596
  65.0 3.0 %copy-start.1 = (bf16[1024,112]{0,1:T(8,128)(2,1)S(1)}, bf16[1024,112]{0,1:T(8,128)(2,1)}, u32[]{:S(2)}) copy-start(bf16[1024,112]{0,1:T(8,128)(2,1)} %param.20) | copy-start | bytes 688132
  65.0 3.2 %copy-start.2 = (bf16[1024,112]{0,1:T(8,128)(2,1)S(1)}, bf16[1024,112]{0,1:T(8,128)(2,1)}, u32[]{:S(2)}) copy-start(bf16[1024,112]{0,1:T(8,128)(2,1)} %param.21) | copy-start | bytes 688132
  68.0 1.3 copy-start.6
  69.2 44.8 %copy-start.5 = (bf16[1024,512]{1,0:T(8,128)(2,1)S(1)}, bf16[1024,512]{1,0:T(8,128)(2,1)}, u32[]{:S(2)}) copy-start(bf16[1024,512]{1,0:T(8,128)(2,1)} %param.14) | copy-start | bytes 3145732
  118.3 0.9 copy-start.3

commit v3 on v2

--- a/solution.py
+++ b/solution.py
@@ -10,6 +10,7 @@
 NO = NX * NC * NY
 BF = jnp.bfloat16
 F32 = jnp.float32
+SECOND, THIRD = 3, 6
 VM = pl.BlockSpec(memory_space=pltpu.VMEM)
 
 
@@ -66,7 +67,7 @@
 
 def line_kernel(
     q_ref, i_ref, picks_ref, embed_ref, out_ref, iout_ref, r3_ref,
-    p1, r1, s2, r2, s3, send_sem, recv_sem, ss1, rs1, ss2, rs2, ss3, rs3,
+    p1, pc, q1, r1, s2, r2, s3, send_sem, recv_sem, sc, rc, ss1, rs1, ss2, rs2, ss3, rs3,
 ):
     ns = NX * NC
     x, z, c, y = here()
@@ -76,6 +77,7 @@
     greet(line_peer, NZ)
     greet(side_peer, ns)
     pl.semaphore_wait(pltpu.get_barrier_semaphore(), NZ + ns - 2)
+    partner = (x, z, 1 - c, y)
 
     def copy(way, step, part):
         place = lax.rem(z + (NZ - step if way == 0 else step), NZ)
@@ -94,9 +96,12 @@
             for h in range(2):
                 p1[place, 2 * f + h] = part[h * 32 : h * 32 + 32, f * 128 : f * 128 + 128]
 
+    def swap(px):
+        return remote(p1.at[px * NC + 1 - c], pc.at[px], sc.at[px], rc.at[px], partner)
+
     def first(k):
-        device, place = side_peer(k)
-        return remote(p1.at[place], r1.at[me], ss1.at[k], rs1.at[k], device)
+        px = lax.rem(x + k, NX)
+        return remote(q1.at[px], r1.at[x], ss1.at[k], rs1.at[k], (px, z, c, y))
 
     def second(k):
         device, place = line_peer(k)
@@ -107,14 +112,9 @@
         return remote(s3, r3_ref.at[z], ss3.at[k], rs3.at[k], device)
 
     def start_second():
-        @pl.loop(1, ns)
-        def _(k):
+        for k in range(1, NX):
             first(k).wait()
-
-        total = r1[0]
-        for j in range(1, ns):
-            total = total + r1[j]
-        s2[...] = total
+        s2[...] = (r1[0] + r1[1]) + (r1[2] + r1[3])
 
         @pl.loop(1, NZ)
         def _(k):
@@ -148,22 +148,31 @@
                     continue
                 started[way, step, part] = copy(way, step, part)
                 started[way, step, part].start()
-        if step < 4:
-
-            @pl.loop(1 + 2 * step, min(3 + 2 * step, ns))
-            def _(k):
-                _, place = side_peer(k)
-                partial(place)
-                first(k).start()
-
-        if step == 3:
-            partial(me)
-            r1[me] = p1[me]
+        if step == 0:
+
+            @pl.loop(0, NX)
+            def _(px):
+                partial(px * NC + 1 - c)
+                swap(px).start()
+
+            @pl.loop(0, NX)
+            def _(px):
+                partial(px * NC + c)
+
+        if step == 1:
+            for k in (2, 1, 3, 0):
+                px = lax.rem(x + k, NX)
+                swap(px).wait()
+                q1[px] = p1[px * NC + c] + pc[px]
+                if k:
+                    first(k).start()
+            r1[x] = q1[x]
             out_ref[z] = q_ref[...]
             iout_ref[z] = i_ref[...]
-        if step == 5:
+        if step == SECOND:
             start_second()
-    start_third()
+        if step == THIRD:
+            start_third()
     for (way, step, part), done in started.items():
         if way == 0 and step == NZ // 2 - 1:
             done.wait_recv()
@@ -188,12 +197,14 @@
         out_specs=(VM, VM, VM),
         scratch_shapes=[
             pltpu.VMEM((ns, NZ, 32, 128), BF),
-            pltpu.VMEM((ns, NZ, 32, 128), BF),
+            pltpu.VMEM((NX, NZ, 32, 128), BF),
+            pltpu.VMEM((NX, NZ, 32, 128), BF),
+            pltpu.VMEM((NX, NZ, 32, 128), BF),
             pltpu.VMEM((NZ, 32, 128), BF),
             pltpu.VMEM((NZ, 32, 128), BF),
             pltpu.VMEM((32, 128), BF),
-            dma((2, NZ // 2, 3)), dma((2, NZ // 2, 3)),
-            dma((ns,)), dma((ns,)), dma((NZ,)), dma((NZ,)), dma((NZ,)), dma((NZ,)),
+            dma((2, NZ // 2, 3)), dma((2, NZ // 2, 3)), dma((NX,)), dma((NX,)),
+            dma((NX,)), dma((NX,)), dma((NZ,)), dma((NZ,)), dma((NZ,)), dma((NZ,)),
         ],
         compiler_params=pltpu.CompilerParams(collective_id=0, has_side_effects=True),
     )(rows, ints, picks, embed)
@@ -359,7 +370,8 @@
     total = r1[0]
     for j in range(1, NO):
         total = total + r1[j]
-    s2[...] = total
+    for i in range(NZ):
+        s2[i] = total[i : i + 1]
     total = c1[0]
     for j in range(1, ns):
         total = total + c1[j]
@@ -403,7 +415,7 @@
         in_specs=[VM, VM],
         out_specs=(VM, VM),
         scratch_shapes=[
-            pltpu.VMEM((NO, NZ, 1, 128), F32),
+            pltpu.VMEM((NO, NZ, 128), F32),
             pltpu.VMEM((NZ, 1, 128), F32),
             pltpu.VMEM((ns, 8, 128), F32),
             pltpu.VMEM((8, 128), F32),
@@ -502,7 +514,7 @@
         jnp.where(odd, logit3[:, :, 1:], logit3[:, :, :1]),
         jnp.where(odd, mass3[:, :, 1:], mass3[:, :, :1]),
     )
-    ret = jnp.where((lane % 64) // 2 == mine, spread, 0.0).reshape(NO, NZ, 1, 128)
+    ret = jnp.where((lane % 64) // 2 == mine, spread, 0.0)
 
     table, token_scores = give_back(ret, score)
     table = table.reshape(NZ, 128)

time: 158 us -> 150 us (0.949)
  Pallas kernels: 123 us -> 118 us
  other arithmetic: 12.1 us -> 10.1 us
    pallas_call x1, Pallas kernels: 43.4 us -> 40.1 us  [exchange(): pl.pallas_call(exchange_kernel, out_shape=(jax.ShapeDtypeStruct(rows.shap...]
    select_n x1, other arithmetic: 3.09 us -> 1.03 us  [body(): ret = jnp.where(lane % 64 // 2 == mine, spread, 0.0)]
where the time goes in v3:
time: 150 us
  Pallas kernels  118 us (79%)
  matrix products  10.5 us (7%)
  other arithmetic  10.1 us (7%)
  local copies, waits for them, and re-layouts  10 us (7%)
    pallas_call x1, Pallas kernels, gather_line(): pl.pallas_call(line_kernel, out_shape=(jax.ShapeDtypeStruct((NZ,) + rows....  54.2 us
    pallas_call x1, Pallas kernels, exchange(): pl.pallas_call(exchange_kernel, out_shape=(jax.ShapeDtypeStruct(rows.shap...  40.1 us
    pallas_call x1, Pallas kernels, give_back(): pl.pallas_call(return_kernel, out_shape=(jax.ShapeDtypeStruct((NZ, 1, 128...  23.7 us
    dot_general x1, matrix products, body(): all_logits = jnp.dot(hidden, class_out, preferred_element_type=F32)  4.29 us
    unnamed x20, local copies, waits for them, and re-layouts  3.6 us
    dot_general x1, matrix products, body(): jnp.einsum('sd,pd->sp', got_rows, passages, preferred_element_type=F32)  3.24 us

profile of v3, /device:TPU:1, one launch (start us, length us, event | category | flops | bytes accessed | tf_op | source)
XLA Modules:
  0.0 149.5 jit_solution(12703180700871364851)
XLA Ops:
  0.7 0.8 broadcast_subtract_fusion
  1.5 0.8 fusion.6.picks_ref
  2.4 0.8 copy.43
  3.2 0.3 convert_reduce_fusion.1
  3.7 0.7 fusion.15
  4.4 0.7 add_bitcast_fusion
  5.1 0.6 pad.22.i_ref
  5.7 54.2 %shard_map.139 = (bf16[16,2,32,768]{3,2,1,0:T(8,128)(2,1)}, s32[16,16,128]{2,1,0:T(8,128)}, bf16[16,32,128]{2,1,0:T(8,128)(2,1)}) custom-call(bf16[2,32,768]{2,1,0:T(8,128)(2,1)} %bitcast.35, s32[16,128]{1,0:T(8,128)} %pad.22.i_ref, bf16[8,64,256]{2,1,0:T(8,128)(2,1)} %fusion.6.picks_ref, bf16[256,1024]{1,0:T(8,128)(2,1)} %embed_ref.1), custom_call_target="tpu_custom_call" | custom-call | tf_op jit(solution)/shard_map/pallas_call | solution.py:189
  59.9 0.9 slice_bitcast_fusion.1
  61.0 0.7 fusion.1
  61.9 1.1 select_reduce_fusion
  62.9 0.6 pad.23
  63.5 0.8 compare_and_fusion
  64.3 3.0 %convolution_convert_fusion = bf16[1024,768]{1,0:T(8,128)(2,1)} fusion(pred[1024,1024]{1,0:T(32,128)(4,1)S(1)} %bitcast.34, bf16[1024,768]{1,0:T(8,128)(2,1)S(1)} %bitcast.45), kind=kOutput, calls=%fused_computation.9 | convolution fusion | flops 1611399168 | bytes 4194304 | tf_op jit(solution)/shard_map/dot_general | solution.py:487
  67.7 0.9 fusion.5.w_ref
  68.6 0.6 broadcast_in_dim.149.ws_ref
  69.2 40.1 %shard_map.140 = (bf16[32,32,768]{2,1,0:T(8,128)(2,1)}, s32[32,1,128]{2,1,0:T(1,128)}, f32[8,128]{1,0:T(8,128)}) custom-call(bf16[32,32,768]{2,1,0:T(8,128)(2,1)} %bitcast.33, s32[32,1,128]{2,1,0:T(1,128)} %bitcast.36, bf16[16,32,128]{2,1,0:T(8,128)(2,1)} %get-tuple-element.13.r3_ref, bf16[1024,256]{1,0:T(8,128)(2,1)} %fusion.5.w_ref, ...), custom_call_target="tpu_custom_call" | custom-call | tf_op jit(solution)/shard_map/pallas_call | solution.py:310
  109.3 0.7 slice_add_fusion
  110.1 4.3 %select_reduce_fusion.4 = f32[1024]{0:T(1024)S(1)} fusion(bf16[1024,512]{1,0:T(8,128)(2,1)S(1)} %copy-done.5, s32[1024]{0:T(1024)S(1)} %sub.68, bf16[1024,768]{1,0:T(8,128)(2,1)} %bitcast.46, bf16[768,1024]{1,0:T(8,128)(2,1)S(1)} %copy-done), kind=kOutput, calls=%fused_computation.6 | convolution fusion | flops 2688023552 | bytes 4202496 | tf_op jit(solution)/shard_map/dot_general | solution.py:498
  114.7 0.2 copy.60
  115.0 0.3 copy.61
  115.3 0.3 reduce-window.9
  116.1 3.2 %select_reduce_fusion.1 = f32[1024]{0:T(1024)S(1)} fusion(bf16[1024,768]{1,0:T(8,128)(2,1)} %bitcast.47, bf16[768,768]{1,0:T(8,128)(2,1)} %param.15, s32[1024]{0:T(1024)S(1)} %sub.68, s32[768]{0:T(1024)S(1)} %convert_reduce_fusion), kind=kOutput, calls=%fused_computation.3 | convolution fusion | flops 1210317824 | bytes 2763776 | tf_op jit(solution)/shard_map/sd,pd->sp/dot_general | solution.py:504
  119.7 0.2 copy.62
  120.0 0.3 copy.63
  120.3 1.0 select_select_fusion.ret_ref
  121.3 23.7 %shard_map.141 = (f32[16,1,128]{2,1,0:T(1,128)}, f32[1,128]{1,0:T(1,128)}) custom-call(f32[32,16,128]{2,1,0:T(8,128)} %select_select_fusion.ret_ref, f32[8,128]{1,0:T(8,128)} %get-tuple-element.16.score_ref), custom_call_target="tpu_custom_call" | custom-call | tf_op jit(solution)/shard_map/pallas_call | solution.py:409
  145.0 0.8 fusion.34
  146.1 0.7 select_reduce_fusion.2
  147.0 0.7 copy.58
  147.7 0.7 copy.59
  148.4 1.1 copy.67
  (50 shorter events, 2.8 us)
Async XLA Ops:
  0.6 109.5 %copy-start = (bf16[768,1024]{1,0:T(8,128)(2,1)S(1)}, bf16[768,1024]{1,0:T(8,128)(2,1)}, u32[]{:S(2)}) copy-start(bf16[768,1024]{1,0:T(8,128)(2,1)} %param.13) | copy-start | bytes 4718596
  61.0 3.3 %copy-start.4 = (bf16[16,2,32,768]{3,2,1,0:T(8,128)(2,1)S(1)}, bf16[16,2,32,768]{3,2,1,0:T(8,128)(2,1)}, u32[]{:S(2)}) copy-start(bf16[16,2,32,768]{3,2,1,0:T(8,128)(2,1)} %get-tuple-element.12) | copy-start | bytes 4718596
  64.3 3.0 %copy-start.1 = (bf16[1024,112]{0,1:T(8,128)(2,1)S(1)}, bf16[1024,112]{0,1:T(8,128)(2,1)}, u32[]{:S(2)}) copy-start(bf16[1024,112]{0,1:T(8,128)(2,1)} %param.20) | copy-start | bytes 688132
  64.3 3.2 %copy-start.2 = (bf16[1024,112]{0,1:T(8,128)(2,1)S(1)}, bf16[1024,112]{0,1:T(8,128)(2,1)}, u32[]{:S(2)}) copy-start(bf16[1024,112]{0,1:T(8,128)(2,1)} %param.21) | copy-start | bytes 688132
  67.3 1.3 copy-start.6
  68.6 41.5 %copy-start.5 = (bf16[1024,512]{1,0:T(8,128)(2,1)S(1)}, bf16[1024,512]{1,0:T(8,128)(2,1)}, u32[]{:S(2)}) copy-start(bf16[1024,512]{1,0:T(8,128)(2,1)} %param.14) | copy-start | bytes 3145732
  114.4 0.9 copy-start.3

commit v4 on v3

--- a/solution.py
+++ b/solution.py
@@ -10,6 +10,7 @@
 NO = NX * NC * NY
 BF = jnp.bfloat16
 F32 = jnp.float32
+STRIDE = 11
 SECOND, THIRD = 3, 6
 VM = pl.BlockSpec(memory_space=pltpu.VMEM)
 
@@ -243,7 +244,7 @@
 
     @pl.loop(1, NO)
     def _(k):
-        for each in copies(k):
+        for each in copies(lax.rem(k * STRIDE, NO)):
             each.start()
 
     out_ref[me] = q_ref[me]

time: 150 us -> 151 us (level)
  no operation moved by 1% of the time
where the time goes in v4:
time: 151 us; the launch traced here: 150 us
  Pallas kernels  119 us (79%)
  matrix products  10.5 us (7%)
  other arithmetic  10.1 us (7%)
  local copies, waits for them, and re-layouts  10 us (7%)
    pallas_call x1, Pallas kernels, gather_line(): pl.pallas_call(line_kernel, out_shape=(jax.ShapeDtypeStruct((NZ,) + rows....  54.2 us
    pallas_call x1, Pallas kernels, exchange(): pl.pallas_call(exchange_kernel, out_shape=(jax.ShapeDtypeStruct(rows.shap...  40.7 us
    pallas_call x1, Pallas kernels, give_back(): pl.pallas_call(return_kernel, out_shape=(jax.ShapeDtypeStruct((NZ, 1, 128...  23.7 us
    dot_general x1, matrix products, body(): all_logits = jnp.dot(hidden, class_out, preferred_element_type=F32)  4.29 us
    unnamed x20, local copies, waits for them, and re-layouts  3.6 us
    dot_general x1, matrix products, body(): jnp.einsum('sd,pd->sp', got_rows, passages, preferred_element_type=F32)  3.24 us

profile of v4, /device:TPU:1, one launch (start us, length us, event | category | flops | bytes accessed | tf_op | source)
XLA Modules:
  0.0 150.1 jit_solution(1916047476314462281)
XLA Ops:
  0.7 0.8 broadcast_subtract_fusion
  1.5 0.8 fusion.6.picks_ref
  2.4 0.8 copy.43
  3.2 0.3 convert_reduce_fusion.1
  3.7 0.7 fusion.15
  4.4 0.7 add_bitcast_fusion
  5.1 0.6 pad.22.i_ref
  5.7 54.2 %shard_map.139 = (bf16[16,2,32,768]{3,2,1,0:T(8,128)(2,1)}, s32[16,16,128]{2,1,0:T(8,128)}, bf16[16,32,128]{2,1,0:T(8,128)(2,1)}) custom-call(bf16[2,32,768]{2,1,0:T(8,128)(2,1)} %bitcast.35, s32[16,128]{1,0:T(8,128)} %pad.22.i_ref, bf16[8,64,256]{2,1,0:T(8,128)(2,1)} %fusion.6.picks_ref, bf16[256,1024]{1,0:T(8,128)(2,1)} %embed_ref.1), custom_call_target="tpu_custom_call" | custom-call | tf_op jit(solution)/shard_map/pallas_call | solution.py:190
  59.9 0.9 slice_bitcast_fusion.1
  61.0 0.7 fusion.1
  61.9 1.1 select_reduce_fusion
  62.9 0.6 pad.23
  63.5 0.8 compare_and_fusion
  64.3 3.0 %convolution_convert_fusion = bf16[1024,768]{1,0:T(8,128)(2,1)} fusion(pred[1024,1024]{1,0:T(32,128)(4,1)S(1)} %bitcast.34, bf16[1024,768]{1,0:T(8,128)(2,1)S(1)} %bitcast.45), kind=kOutput, calls=%fused_computation.9 | convolution fusion | flops 1611399168 | bytes 4194304 | tf_op jit(solution)/shard_map/dot_general | solution.py:488
  67.7 0.9 fusion.5.w_ref
  68.6 0.6 broadcast_in_dim.149.ws_ref
  69.2 40.7 %shard_map.140 = (bf16[32,32,768]{2,1,0:T(8,128)(2,1)}, s32[32,1,128]{2,1,0:T(1,128)}, f32[8,128]{1,0:T(8,128)}) custom-call(bf16[32,32,768]{2,1,0:T(8,128)(2,1)} %bitcast.33, s32[32,1,128]{2,1,0:T(1,128)} %bitcast.36, bf16[16,32,128]{2,1,0:T(8,128)(2,1)} %get-tuple-element.13.r3_ref, bf16[1024,256]{1,0:T(8,128)(2,1)} %fusion.5.w_ref, ...), custom_call_target="tpu_custom_call" | custom-call | tf_op jit(solution)/shard_map/pallas_call | solution.py:311
  109.8 0.7 slice_add_fusion
  110.6 4.3 %select_reduce_fusion.4 = f32[1024]{0:T(1024)S(1)} fusion(bf16[1024,512]{1,0:T(8,128)(2,1)S(1)} %copy-done.5, s32[1024]{0:T(1024)S(1)} %sub.68, bf16[1024,768]{1,0:T(8,128)(2,1)} %bitcast.46, bf16[768,1024]{1,0:T(8,128)(2,1)S(1)} %copy-done), kind=kOutput, calls=%fused_computation.6 | convolution fusion | flops 2688023552 | bytes 4202496 | tf_op jit(solution)/shard_map/dot_general | solution.py:499
  115.3 0.2 copy.60
  115.5 0.3 copy.61
  115.8 0.3 reduce-window.9
  116.7 3.2 %select_reduce_fusion.1 = f32[1024]{0:T(1024)S(1)} fusion(bf16[1024,768]{1,0:T(8,128)(2,1)} %bitcast.47, bf16[768,768]{1,0:T(8,128)(2,1)} %param.15, s32[1024]{0:T(1024)S(1)} %sub.68, s32[768]{0:T(1024)S(1)} %convert_reduce_fusion), kind=kOutput, calls=%fused_computation.3 | convolution fusion | flops 1210317824 | bytes 2763776 | tf_op jit(solution)/shard_map/sd,pd->sp/dot_general | solution.py:505
  120.2 0.2 copy.62
  120.5 0.3 copy.63
  120.8 1.0 select_select_fusion.ret_ref
  121.8 23.7 %shard_map.141 = (f32[16,1,128]{2,1,0:T(1,128)}, f32[1,128]{1,0:T(1,128)}) custom-call(f32[32,16,128]{2,1,0:T(8,128)} %select_select_fusion.ret_ref, f32[8,128]{1,0:T(8,128)} %get-tuple-element.16.score_ref), custom_call_target="tpu_custom_call" | custom-call | tf_op jit(solution)/shard_map/pallas_call | solution.py:410
  145.6 0.8 fusion.34
  146.7 0.7 select_reduce_fusion.2
  147.6 0.7 copy.58
  148.3 0.7 copy.59
  149.0 1.1 copy.67
  (50 shorter events, 2.8 us)
Async XLA Ops:
  0.6 110.0 %copy-start = (bf16[768,1024]{1,0:T(8,128)(2,1)S(1)}, bf16[768,1024]{1,0:T(8,128)(2,1)}, u32[]{:S(2)}) copy-start(bf16[768,1024]{1,0:T(8,128)(2,1)} %param.13) | copy-start | bytes 4718596
  61.0 3.3 %copy-start.4 = (bf16[16,2,32,768]{3,2,1,0:T(8,128)(2,1)S(1)}, bf16[16,2,32,768]{3,2,1,0:T(8,128)(2,1)}, u32[]{:S(2)}) copy-start(bf16[16,2,32,768]{3,2,1,0:T(8,128)(2,1)} %get-tuple-element.12) | copy-start | bytes 4718596
  64.3 3.0 %copy-start.1 = (bf16[1024,112]{0,1:T(8,128)(2,1)S(1)}, bf16[1024,112]{0,1:T(8,128)(2,1)}, u32[]{:S(2)}) copy-start(bf16[1024,112]{0,1:T(8,128)(2,1)} %param.20) | copy-start | bytes 688132
  64.3 3.2 %copy-start.2 = (bf16[1024,112]{0,1:T(8,128)(2,1)S(1)}, bf16[1024,112]{0,1:T(8,128)(2,1)}, u32[]{:S(2)}) copy-start(bf16[1024,112]{0,1:T(8,128)(2,1)} %param.21) | copy-start | bytes 688132
  67.3 1.3 copy-start.6
  68.6 42.1 %copy-start.5 = (bf16[1024,512]{1,0:T(8,128)(2,1)S(1)}, bf16[1024,512]{1,0:T(8,128)(2,1)}, u32[]{:S(2)}) copy-start(bf16[1024,512]{1,0:T(8,128)(2,1)} %param.14) | copy-start | bytes 3145732
  114.9 0.9 copy-start.3
